TPU v7x, 32 devices: a whole 2x2x4 slice. The times are simulated.
32 devices in a mesh: wide: 8 (over z, x), narrow: 4 (over y, core).
Axes of the slice: x: 2, y: 2, z: 4, core: 2. Of those that a mesh axis runs over, the one named last changes fastest.
Arguments:
- hidden: bfloat16 [512, 4096], P('narrow', 'wide'), may hold values from -6 to 6
- attn_gain: float32 [4096], replicated, may hold values from 0.5 to 1.5
- query_weight: bfloat16 [4096, 4096], P(None, 'wide'), may hold values from -0.09375 to 0.09375
- key_weight: bfloat16 [4096, 1024], P('wide'), may hold values from -0.125 to 0.125
- value_weight: bfloat16 [4096, 1024], P('wide'), may hold values from -0.125 to 0.125
- out_weight: bfloat16 [4096, 4096], P('wide'), may hold values from -0.09375 to 0.09375
- cache_key: bfloat16 [8, 512, 128], replicated, may hold values from -600 to 600
- cache_value: bfloat16 [8, 512, 128], replicated, may hold values from -6 to 6
- mlp_gain: float32 [4096], replicated, may hold values from 0.5 to 1.5
- router_weight: bfloat16 [4096, 16], replicated, may hold values from -0.09375 to 0.09375
- expert_ids: int32 [512, 2], P('narrow'), may hold values from 0 to 15, all different within a row; in each aligned block of 16 rows (0 to 15, 16 to 31, ...) at most 4 rows name the same one
- gate_weight: bfloat16 [32, 4096, 3200], P('wide', None, 'narrow'), may hold values from -0.09375 to 0.09375
- up_weight: bfloat16 [32, 4096, 3200], P('wide', None, 'narrow'), may hold values from -0.09375 to 0.09375
- down_weight: bfloat16 [32, 3200, 4096], P('wide', 'narrow'), may hold values from -0.078125 to 0.078125
Outputs:
- layer_out: bfloat16 [512, 4096], P('narrow', 'wide')
Inputs may be any that keep to these rules, and one draw needn't show every extreme that they name: `expert_ids`: in each aligned block of 16 rows no expert is named by more than 4 rows, and in every block some expert by exactly 4; the two experts of a row differ.
All inputs are finite; a program needn't handle non-finite values.
Results may differ from a plain program's by a relative error of at most 0.012.
The roundings to bfloat16 on the way count: a program that leaves them out, or rounds other values in their place, can miss the bound.
Values may be sent and summed in bfloat16 or wider, within the bound.
No kernel may reach another device: no remote copies, remote signals or barrier semaphores. Data moves between devices by JAX's collectives and lax.ppermute only.
A program may use at most 192 MiB of HBM per device.

v0:
```python
import jax
import jax.numpy as jnp
import numpy as np
from jax import lax
from jax.experimental import pallas as pl
from jax.experimental.pallas import tpu as pltpu
from jax.sharding import PartitionSpec as P


SPLIT = 2
CAPD = 4
TOK_BLOCK = 16
DIRECT_LIMIT = 8
UNIT_BLOCK = 400
MIX_CHUNKS = 2
SMALL_VMEM = 24 << 20


epsilon = 1e-05


def swap(values, axis, distance):
    count = lax.axis_size(axis)
    return lax.ppermute(values, axis, [(i, i ^ distance) for i in range(count)])


def is_power_of_two(count):
    return count & (count - 1) == 0


def owners_by_distance(axis):
    count = lax.axis_size(axis)
    owners = jnp.arange(count, dtype=jnp.int32)
    return lax.axis_index(axis) ^ owners if travels_directly(axis) else owners


def travels_directly(axis):
    count = lax.axis_size(axis)
    return 2 <= count <= DIRECT_LIMIT and is_power_of_two(count)


def gather_blocks(values, axis):
    count = lax.axis_size(axis)
    if not travels_directly(axis):
        gathered = lax.all_gather(values, axis, axis=0)
        return [gathered[i] for i in range(count)]
    held = {0: values}
    for distance in range(2, count, 2):
        held[distance] = swap(values, axis, distance)
    for distance in range(1, count, 2):
        held[distance] = swap(held[distance - 1], axis, 1)
    return [held[distance] for distance in range(count)]


def sum_blocks(far, near, axis):
    f32, bf16 = jnp.float32, jnp.bfloat16
    count = lax.axis_size(axis)
    if not travels_directly(axis):
        terms = lax.all_to_all(
            jnp.concatenate([far, near]), axis, split_axis=0, concat_axis=0, tiled=True
        )
        return jnp.sum(terms.astype(f32), axis=0)
    arrived = swap(far, axis, 1)
    total = near[0].astype(f32) + arrived[0].astype(f32)
    for i in range(1, count // 2):
        term = (near[i].astype(f32) + arrived[i].astype(f32)).astype(bf16)
        total = total + swap(term, axis, 2 * i).astype(f32)
    return total


def split_order(axis):
    count = lax.axis_size(axis)
    positions = list(range(count))
    if travels_directly(axis):
        return positions[1::2], positions[0::2]
    return positions[: count // 2], positions[count // 2 :]


SMEM_SPEC = pl.BlockSpec(memory_space=pltpu.SMEM)
VMEM_SPEC = pl.BlockSpec(memory_space=pltpu.VMEM)


def row_statistics(blocks, features):
    rows = blocks[0].shape[0]
    total = jnp.zeros((rows, 1), jnp.float32)
    for block in blocks:
        total += jnp.sum(block[...].astype(jnp.float32), axis=1, keepdims=True)
    average = total / features
    square = jnp.zeros((rows, 1), jnp.float32)
    for block in blocks:
        centered = block[...].astype(jnp.float32) - average
        square += jnp.sum(centered * centered, axis=1, keepdims=True)
    return average, lax.rsqrt(square / features + epsilon)


def key_value_terms(blocks, own, gain, key_weight, value_weight, order, group_of, head_size, kv_width):
    f32, bf16 = jnp.float32, jnp.bfloat16
    rows, share = own.shape
    count = len(blocks)
    far, near = split_order("wide")
    columns = key_weight.shape[1] // head_size
    heads = kv_width // head_size

    def kernel(*refs):
        order_ref, group_ref, own_ref, gain_ref, k_ref, v_ref = refs[:6]
        block_refs = refs[6 : 6 + count]
        far_ref, near_ref, mean_ref, scale_ref, terms = refs[6 + count :]
        average, scale = row_statistics(block_refs, share * count)
        mean_ref[...] = average
        scale_ref[...] = scale
        n = ((own_ref[...].astype(f32) - average) * scale * gain_ref[...]).astype(bf16)
        for which, ref in enumerate((k_ref, v_ref)):
            term = jnp.dot(n, ref[...], preferred_element_type=f32).astype(bf16)
            for c in range(columns):
                terms[which, c] = term[:, c * head_size : (c + 1) * head_size]
        for out_ref, positions in ((far_ref, far), (near_ref, near)):
            for i, position in enumerate(positions):
                first = group_ref[order_ref[position]]
                for which in range(2):
                    for h in range(heads):
                        out_ref[i, which, :, h * head_size : (h + 1) * head_size] = terms[
                            which, first + h
                        ]

    half = jax.ShapeDtypeStruct((count // 2, 2, rows, kv_width), bf16)
    column = jax.ShapeDtypeStruct((rows, 1), f32)
    return pl.pallas_call(
        kernel,
        in_specs=[SMEM_SPEC] * 2 + [VMEM_SPEC] * (4 + count),
        out_specs=[VMEM_SPEC] * 4,
        out_shape=[half, half, column, column],
        scratch_shapes=[pltpu.VMEM((2, columns, rows, head_size), bf16)],
        compiler_params=pltpu.CompilerParams(vmem_limit_bytes=SMALL_VMEM),
        name="kv_terms",
    )(order, group_of, own, gain, key_weight, value_weight, *blocks)


def query_rows(blocks, average, scale, gain, query_weight, order):
    f32, bf16 = jnp.float32, jnp.bfloat16
    rows, share = blocks[0].shape
    count = len(blocks)
    width = query_weight.shape[1]

    def kernel(*refs):
        order_ref, mean_ref, scale_ref, gain_ref, w_ref = refs[:5]
        block_refs = refs[5 : 5 + count]
        out_ref, acc = refs[5 + count :]
        for k in range(count):
            owner = order_ref[k]
            n = (block_refs[k][...].astype(f32) - mean_ref[...]) * scale_ref[...] * gain_ref[owner]
            at = pl.multiple_of(owner * share, share)
            term = jnp.dot(n.astype(bf16), w_ref[pl.ds(at, share), :], preferred_element_type=f32)
            if k == 0:
                acc[...] = term
            else:
                acc[...] += term
        out_ref[...] = acc[...].astype(bf16)

    return pl.pallas_call(
        kernel,
        in_specs=[SMEM_SPEC] + [VMEM_SPEC] * (4 + count),
        out_specs=VMEM_SPEC,
        out_shape=jax.ShapeDtypeStruct((rows, width), bf16),
        scratch_shapes=[pltpu.VMEM((rows, width), f32)],
        compiler_params=pltpu.CompilerParams(vmem_limit_bytes=SMALL_VMEM),
        name="queries",
    )(order, average, scale, gain.reshape(count, 1, share), query_weight, *blocks)


def mix_terms(attended, out_weight, order, chunks):
    f32, bf16 = jnp.float32, jnp.bfloat16
    rows = attended.shape[0]
    count = order.shape[0]
    share = out_weight.shape[1] // count
    far, near = split_order("wide")
    half, chunk = count // 2, rows // chunks

    def kernel(order_ref, a_ref, w_ref, *out_refs):
        a = a_ref[...]
        for side, positions in enumerate((far, near)):
            for i, position in enumerate(positions):
                at = pl.multiple_of(order_ref[position] * share, share)
                term = jnp.dot(a, w_ref[:, pl.ds(at, share)], preferred_element_type=f32)
                for c in range(chunks):
                    out_refs[side * chunks + c][i] = term[c * chunk : (c + 1) * chunk].astype(bf16)

    outs = pl.pallas_call(
        kernel,
        in_specs=[SMEM_SPEC] + [VMEM_SPEC] * 2,
        out_specs=[VMEM_SPEC] * (2 * chunks),
        out_shape=[jax.ShapeDtypeStruct((half, chunk, share), bf16)] * (2 * chunks),
        compiler_params=pltpu.CompilerParams(vmem_limit_bytes=SMALL_VMEM),
        name="mix_terms",
    )(order, attended, out_weight)
    return outs[:chunks], outs[chunks:]


def normed_rows(got, gain):
    owners, rows, share = got.shape
    features = owners * share

    def kernel(x_ref, g_ref, out_ref):
        total = jnp.zeros((rows, 1), jnp.float32)
        for o in range(owners):
            total += jnp.sum(x_ref[o].astype(jnp.float32), axis=1, keepdims=True)
        average = total / features
        square = jnp.zeros((rows, 1), jnp.float32)
        for o in range(owners):
            centered = x_ref[o].astype(jnp.float32) - average
            square += jnp.sum(centered * centered, axis=1, keepdims=True)
        scale = lax.rsqrt(square / features + epsilon)
        for o in range(owners):
            at = slice(o * share, (o + 1) * share)
            centered = x_ref[o].astype(jnp.float32) - average
            out_ref[:, at] = (centered * scale * g_ref[:, at]).astype(jnp.bfloat16)

    return pl.pallas_call(
        kernel,
        out_shape=jax.ShapeDtypeStruct((rows, features), jnp.bfloat16),
        compiler_params=pltpu.CompilerParams(vmem_limit_bytes=SMALL_VMEM),
        name="normed_rows",
    )(got, gain.reshape(1, -1))


def expert_partial(pieces, gate_weight, up_weight, down_weight, first, parts):
    f32, bf16 = jnp.float32, jnp.bfloat16
    rows = sum(piece.shape[0] for piece in pieces)
    units, features = gate_weight.shape[1:]
    half = rows // 2
    block = max(b for b in range(16, units + 1, 16) if units % b == 0 and b <= UNIT_BLOCK)
    steps = units // block
    by_rows = (((1,), (1,)), ((), ()))

    def kernel(*refs):
        piece_refs = refs[: len(pieces)]
        g_ref, u_ref, d_ref, keep, send, x, acc = refs[len(pieces) :]
        p, s = pl.program_id(0), pl.program_id(1)
        starts = (p == 0) & (s == 0)

        @pl.when(starts)
        def _():
            at = 0
            for ref in piece_refs:
                x[at : at + ref.shape[0], :] = ref[...]
                at += ref.shape[0]

        tokens = x[...]
        gate = lax.dot_general(tokens, g_ref[0], by_rows, preferred_element_type=f32)
        up = lax.dot_general(tokens, u_ref[0], by_rows, preferred_element_type=f32)
        act = (jax.nn.silu(gate) * up).astype(bf16)
        out = jnp.dot(act, d_ref[0], preferred_element_type=f32)

        @pl.when(starts)
        def _():
            acc[...] = out

        @pl.when(jnp.logical_not(starts))
        def _():
            acc[...] += out

        @pl.when((p == parts - 1) & (s == steps - 1))
        def _():
            keep[...] = acc[:half].astype(bf16)
            send[...] = acc[half:].astype(bf16)

    weight_spec = pl.BlockSpec((1, block, features), lambda p, s: (first + p, s, 0))
    out_spec = pl.BlockSpec((half, features), lambda p, s: (0, 0))
    return pl.pallas_call(
        kernel,
        grid=(parts, steps),
        in_specs=[pl.BlockSpec(piece.shape, lambda p, s: (0, 0)) for piece in pieces]
        + [weight_spec] * 3,
        out_specs=[out_spec, out_spec],
        out_shape=[jax.ShapeDtypeStruct((half, features), bf16)] * 2,
        scratch_shapes=[pltpu.VMEM((rows, features), bf16), pltpu.VMEM((rows, features), f32)],
        compiler_params=pltpu.CompilerParams(
            dimension_semantics=("arbitrary", "arbitrary"), vmem_limit_bytes=48 << 20
        ),
        cost_estimate=pl.CostEstimate(
            flops=rows * features * units * 6 * parts,
            bytes_accessed=parts * 3 * features * units * 2,
            transcendentals=rows * units * parts,
        ),
        name="experts",
    )(*pieces, gate_weight, up_weight, down_weight)


def slot_targets(routing, experts, capacity):
    blocks = routing.shape[0]
    flat_ids = routing.reshape(blocks, -1)
    onehot = (flat_ids[:, :, None] == jnp.arange(experts, dtype=jnp.int32)[None, None, :]).astype(
        jnp.int32
    )
    earlier = jnp.cumsum(onehot, axis=1) - onehot
    position = jnp.sum(earlier * onehot, axis=2)
    return (flat_ids * capacity + position).reshape(routing.shape)


def attend(queries, all_keys, all_values, first_row, context):
    row_count, heads_here, head_size = queries.shape
    kv_here = all_keys.shape[0]
    grouped = queries.reshape(row_count, kv_here, heads_here // kv_here, head_size)
    scale_factor = head_size ** (-0.5)
    scores = (
        jnp.einsum("rgqd,gkd->gqrk", grouped, all_keys, preferred_element_type=jnp.float32)
        * scale_factor
    )
    row_ids = first_row + jnp.arange(row_count, dtype=jnp.int32)
    key_ids = jnp.arange(all_keys.shape[1], dtype=jnp.int32) - context
    allowed = key_ids[None, :] <= row_ids[:, None]
    scores = jnp.where(allowed[None, None], scores, -1e30)
    highest = jnp.max(scores, axis=3, keepdims=True)
    weights = jnp.exp(scores - highest)
    weights = (weights / jnp.sum(weights, axis=3, keepdims=True)).astype(jnp.bfloat16)
    mixed = jnp.einsum(
        "gqrk,gkd->rgqd", weights, all_values, preferred_element_type=jnp.float32
    ).astype(jnp.bfloat16)
    return mixed.reshape(row_count, heads_here, head_size)


def gather_pieces(rows):
    count = lax.axis_size("narrow")
    if not is_power_of_two(count) or count < 2:
        raise ValueError("narrow")
    held = {0: rows}
    distance = count // 2
    while distance >= 1:
        for have in sorted(held):
            held[have + distance] = swap(held[have], "narrow", distance)
        distance //= 2
    order = sorted(held, key=lambda d: (d & 1, d))
    return [held[d] for d in order]


def after(values, *others):
    return lax.optimization_barrier((values,) + others)[0]


def start_narrow_sum(keep, send):
    return keep.astype(jnp.float32) + swap(send, "narrow", 1).astype(jnp.float32)


def split_rows(total):
    half = total.shape[0] // 2
    return total[:half], total[half:].astype(jnp.bfloat16)


def body(
    hidden,
    attn_gain,
    query_weight,
    key_weight,
    value_weight,
    out_weight,
    cache_key,
    cache_value,
    mlp_gain,
    router_weight,
    expert_ids,
    gate_weight,
    up_weight,
    down_weight,
):
    f32, bf16 = jnp.float32, jnp.bfloat16
    wide_count = lax.axis_size("wide")
    wide_index = lax.axis_index("wide")
    narrow_index = lax.axis_index("narrow")
    narrow_count = lax.axis_size("narrow")
    row_count, feature_share = hidden.shape
    kv_total, context, head_size = cache_key.shape
    heads_here = query_weight.shape[1] // head_size
    share = heads_here * wide_count // kv_total
    kv_here = max(heads_here // share, 1)
    kv_start = wide_index * heads_here // share

    experts = router_weight.shape[1]
    slots_here = gate_weight.shape[0]
    experts_here = max(slots_here // SPLIT, 1)
    parts_here = slots_here // experts_here
    blocks = row_count // TOK_BLOCK
    routing = expert_ids.reshape(blocks, TOK_BLOCK, 2)
    target = slot_targets(routing, experts, CAPD).reshape(row_count, 2)
    token_block = np.arange(row_count) // TOK_BLOCK
    dest_expert = (np.arange(wide_count)[:, None] * slots_here) // SPLIT + np.arange(experts_here)
    slot_of_row = np.broadcast_to(
        dest_expert[:, :, None, None] * CAPD + np.arange(CAPD),
        (wide_count, experts_here, blocks, CAPD),
    ).reshape(-1)
    block_of_row = np.broadcast_to(
        np.arange(blocks)[:, None], (wide_count, experts_here, blocks, CAPD)
    ).reshape(-1)
    row_slot = jnp.asarray(slot_of_row, jnp.int32)[:, None]
    same_block = jnp.asarray(block_of_row, jnp.int32)[:, None] == jnp.asarray(
        token_block, jnp.int32
    )
    first_pick = (row_slot == target[:, 0][None, :]) & same_block
    second_pick = (row_slot == target[:, 1][None, :]) & same_block
    picks = (first_pick | second_pick).astype(bf16)

    order = owners_by_distance("wide")
    gathered = gather_blocks(hidden, "wide")
    own_gain = lax.dynamic_slice_in_dim(attn_gain, wide_index * feature_share, feature_share, 0)
    kv_width = kv_here * head_size
    group_of = jnp.arange(wide_count, dtype=jnp.int32) * heads_here // share
    far_kv, near_kv, average, scale = key_value_terms(
        gathered,
        hidden,
        own_gain.reshape(1, -1),
        key_weight,
        value_weight,
        order,
        group_of,
        head_size,
        kv_width,
    )
    fresh = sum_blocks(far_kv, near_kv, "wide").astype(bf16)
    queries = query_rows(gathered, average, scale, attn_gain, query_weight, order)
    span = lax.all_gather(fresh, "narrow", axis=1, tiled=True)
    span = span.reshape(2, -1, kv_here, head_size).transpose(0, 2, 1, 3)
    own_cache_key = lax.dynamic_slice_in_dim(cache_key, kv_start, kv_here, 0)
    own_cache_value = lax.dynamic_slice_in_dim(cache_value, kv_start, kv_here, 0)
    all_keys = jnp.concatenate([own_cache_key, span[0]], axis=1)
    all_values = jnp.concatenate([own_cache_value, span[1]], axis=1)
    attended = attend(
        queries.reshape(row_count, heads_here, head_size),
        all_keys,
        all_values,
        narrow_index * row_count,
        context,
    ).reshape(row_count, heads_here * head_size)
    far_mix, near_mix = mix_terms(attended, out_weight, order, MIX_CHUNKS)
    mixed = [sum_blocks(far, near, "wide") for far, near in zip(far_mix, near_mix)]
    residual = (hidden.astype(f32) + jnp.concatenate(mixed)).astype(bf16)

    expert_rows = blocks * CAPD
    picks = picks.reshape(wide_count, experts_here, expert_rows, row_count)
    first_pick = first_pick.astype(f32).reshape(wide_count, experts_here, expert_rows, row_count)
    second_pick = second_pick.astype(f32).reshape(wide_count, experts_here, expert_rows, row_count)
    mine = lambda values: lax.dynamic_index_in_dim(values, wide_index, 0, keepdims=False)
    my_first, my_second = mine(first_pick), mine(second_pick)
    ids_onehot = (expert_ids[:, :, None] == jnp.arange(experts, dtype=jnp.int32)).astype(f32)
    ids_diff = ids_onehot[:, 0] - ids_onehot[:, 1]

    def choose(e):
        return jnp.dot(
            picks[:, e].reshape(wide_count * expert_rows, row_count),
            residual,
            preferred_element_type=f32,
        ).astype(bf16)

    def exchange(blocks_of):
        return lax.all_to_all(blocks_of, "wide", split_axis=0, concat_axis=0, tiled=True)

    def weights_of(e, normed_two):
        logits = jnp.dot(normed_two, router_weight, preferred_element_type=f32)
        ids = jnp.dot(my_first[e] + my_second[e], ids_diff)
        leading = jax.nn.sigmoid(jnp.sum(logits * ids, axis=1))
        return jnp.where(jnp.sum(my_first[e], axis=1) > 0, leading, 1.0 - leading)

    def finish(e, own, other, distance):
        while True:
            own = own + swap(other, "narrow", distance).astype(f32)
            distance //= 2
            if distance < 2:
                break
            own, other = split_rows(own)
        weighted = (own * row_weights[e][:, None]).astype(bf16)
        back = exchange(
            weighted.reshape(expert_rows, wide_count, feature_share).transpose(1, 0, 2)
        )
        return lax.dot_general(
            picks[:, e].reshape(wide_count * expert_rows, row_count),
            back.reshape(-1, feature_share),
            (((0,), (0,)), ((), ())),
            preferred_element_type=f32,
        )

    gate_rows, up_rows = jnp.swapaxes(gate_weight, 1, 2), jnp.swapaxes(up_weight, 1, 2)
    arrived = []
    for e in range(experts_here):
        chosen = choose(e).reshape(wide_count, expert_rows, feature_share)
        arrived.append(exchange(after(chosen, *arrived[-1:])))
    normed_two = [normed_rows(got, mlp_gain) for got in arrived]
    row_weights = [weights_of(e, normed_two[e]) for e in range(experts_here)]
    pieces = [gather_pieces(rows) for rows in normed_two]
    result = residual.astype(f32)
    waiting = normed_two[1:2]
    sums = []
    for e in range(experts_here):
        tokens = [after(pieces[e][0], *waiting)] + pieces[e][1:]
        keep, far_rows = expert_partial(
            tokens, gate_rows, up_rows, down_weight, e * parts_here, parts_here
        )
        own, other = split_rows(start_narrow_sum(keep, far_rows))
        waiting = [other]
        sums.append((own, other))
    for e in range(experts_here):
        result = result + finish(e, *sums[e], narrow_count // 2)
    return result.astype(bf16)


def solution(mesh):
    placed = (
        P("narrow", "wide"),
        P(),
        P(None, "wide"),
        P("wide", None),
        P("wide", None),
        P("wide", None),
        P(),
        P(),
        P(),
        P(),
        P("narrow", None),
        P("wide", None, "narrow"),
        P("wide", None, "narrow"),
        P("wide", "narrow", None),
    )


    return jax.shard_map(
        body, mesh=mesh, in_specs=placed, out_specs=P("narrow", "wide"), check_vma=False
    )
```

profile of v0, /device:TPU:0, one launch (start us, length us, event | category | flops | bytes accessed | tf_op | source)
XLA Modules:
  0.0 184.8 jit_solution(14859930901513004322)
XLA Ops:
  0.0 3.0 %collective-permute-start = (bf16[128,512]{1,0:T(8,128)(2,1)}, bf16[128,512]{1,0:T(8,128)(2,1)S(1)}, u32[]{:S(2)}, u32[]{:S(2)}) collective-permute-start(bf16[128,512]{1,0:T(8,128)(2,1)} %refs_5_.3), channel_id=1, source_target_pairs={{0,4},{4,0},{8,12},{12,8},{16,20},{20,16},{24,28},{28,24},{1,5},{5... | collective-permute-start | bytes 393224 | tf_op jit(solution)/shard_map/ppermute | solution.py:24
  4.5 2.6 %collective-permute-start.3 = (bf16[128,512]{1,0:T(8,128)(2,1)}, bf16[128,512]{1,0:T(8,128)(2,1)S(1)}, u32[]{:S(2)}, u32[]{:S(2)}) collective-permute-start(bf16[128,512]{1,0:T(8,128)(2,1)} %refs_5_.3), channel_id=1, source_target_pairs={{0,16},{4,20},{8,24},{12,28},{16,0},{20,4},{24,8},{28,12},{1,17},{... | collective-permute-start | bytes 393224 | tf_op jit(solution)/shard_map/ppermute | solution.py:24
  10.4 7.0 %collective-permute-done.3.refs_10_.refs_9_ = bf16[128,512]{1,0:T(8,128)(2,1)S(1)} collective-permute-done((bf16[128,512]{1,0:T(8,128)(2,1)}, bf16[128,512]{1,0:T(8,128)(2,1)S(1)}, u32[]{:S(2)}, u32[]{:S(2)}) %collective-permute-start.3) | collective-permute-done | bytes 131104 | tf_op jit(solution)/shard_map/ppermute | solution.py:24
  20.3 2.1 %collective-permute-done.4.refs_11_.refs_10_ = bf16[128,512]{1,0:T(8,128)(2,1)S(1)} collective-permute-done((bf16[128,512]{1,0:T(8,128)(2,1)S(1)}, bf16[128,512]{1,0:T(8,128)(2,1)S(1)}, u32[]{:S(2)}, u32[]{:S(2)}) %collective-permute-start.4) | collective-permute-done | bytes 131104 | tf_op jit(solution)/shard_map/ppermute | solution.py:24
  29.7 5.5 %collective-permute-done.7 = bf16[4,2,128,128]{3,2,1,0:T(8,128)(2,1)S(1)} collective-permute-done((bf16[4,2,128,128]{3,2,1,0:T(8,128)(2,1)S(1)}, bf16[4,2,128,128]{3,2,1,0:T(8,128)(2,1)S(1)}, u32[]{:S(2)}, u32[]{:S(2)}) %collective-permute-start.7) | collective-permute-done | bytes 262176 | tf_op jit(solution)/shard_map/ppermute | solution.py:24
  35.2 2.4 %collective-permute-start.10 = (bf16[2,128,128]{2,1,0:T(8,128)(2,1)S(1)}, bf16[2,128,128]{2,1,0:T(8,128)(2,1)S(1)}, u32[]{:S(2)}, u32[]{:S(2)}) collective-permute-start(bf16[2,128,128]{2,1,0:T(8,128)(2,1)S(1)} %get-tuple-element.44), channel_id=1, source_target_pairs={{0,24},{4,28},{8,16},{12,20},{16,8},{20,12},{24,0},{28,4},{1,25},{... | collective-permute-start | bytes 196616 | tf_op jit(solution)/shard_map/ppermute | solution.py:24
  43.5 5.8 %all_gather.3 = bf16[2,512,128]{2,1,0:T(8,128)(2,1)S(1)} all-gather(bf16[2,128,128]{2,1,0:T(8,128)(2,1)S(1)} %fusion.23), channel_id=1, replica_groups=mesh['wide'=8,'narrow'=4] {'narrow'}, dimensions={1}, use_global_device_ids=true | all-gather | bytes 327680 | tf_op jit(solution)/shard_map/all_gather | solution.py:418
  50.7 2.2 %copy-done.3 = bf16[512,4096]{1,0:T(8,128)(2,1)S(1)} copy-done((bf16[512,4096]{1,0:T(8,128)(2,1)S(1)}, bf16[512,4096]{1,0:T(8,128)(2,1)}, u32[]{:S(2)}) %copy-start.3) | copy-done | bytes 4194328
  56.6 6.9 %collective-permute-done.15 = bf16[4,64,512]{2,1,0:T(8,128)(2,1)S(1)} collective-permute-done((bf16[4,64,512]{2,1,0:T(8,128)(2,1)S(1)}, bf16[4,64,512]{2,1,0:T(8,128)(2,1)S(1)}, u32[]{:S(2)}, u32[]{:S(2)}) %collective-permute-start.15) | collective-permute-done | bytes 262176 | tf_op jit(solution)/shard_map/ppermute | solution.py:24
  65.6 2.4 %collective-permute-start.16 = (bf16[64,512]{1,0:T(8,128)(2,1)S(1)}, bf16[64,512]{1,0:T(8,128)(2,1)S(1)}, u32[]{:S(2)}, u32[]{:S(2)}) collective-permute-start(bf16[64,512]{1,0:T(8,128)(2,1)S(1)} %get-tuple-element.40), channel_id=1, source_target_pairs={{0,8},{4,12},{8,0},{12,4},{16,24},{20,28},{24,16},{28,20},{1,9},{5... | collective-permute-start | bytes 196616 | tf_op jit(solution)/shard_map/ppermute | solution.py:24
  70.6 2.4 %collective-permute-start.12 = (bf16[64,512]{1,0:T(8,128)(2,1)S(1)}, bf16[64,512]{1,0:T(8,128)(2,1)S(1)}, u32[]{:S(2)}, u32[]{:S(2)}) collective-permute-start(bf16[64,512]{1,0:T(8,128)(2,1)S(1)} %get-tuple-element.37), channel_id=1, source_target_pairs={{0,8},{4,12},{8,0},{12,4},{16,24},{20,28},{24,16},{28,20},{1,9},{5... | collective-permute-start | bytes 196616 | tf_op jit(solution)/shard_map/ppermute | solution.py:24
  75.1 2.3 %collective-permute-done.13 = bf16[64,512]{1,0:T(8,128)(2,1)S(1)} collective-permute-done((bf16[64,512]{1,0:T(8,128)(2,1)S(1)}, bf16[64,512]{1,0:T(8,128)(2,1)S(1)}, u32[]{:S(2)}, u32[]{:S(2)}) %collective-permute-start.13) | collective-permute-done | bytes 65568 | tf_op jit(solution)/shard_map/ppermute | solution.py:24
  78.4 3.4 %all-to-all-start = ((bf16[8,32,512]{2,1,0:T(8,128)(2,1)}), bf16[8,32,512]{2,1,0:T(8,128)(2,1)S(1)}, u32[]{:S(2)}, u32[]{:S(2)}) async-start(bf16[8,32,512]{2,1,0:T(8,128)(2,1)} %bitcast.27), calls=%async_computation | async-start | bytes 524288 | tf_op jit(solution)/shard_map/all_to_all | solution.py:452
  82.7 7.9 %all-to-all-done.x_ref = bf16[8,32,512]{2,1,0:T(8,128)(2,1)S(1)} async-done(((bf16[8,32,512]{2,1,0:T(8,128)(2,1)}), bf16[8,32,512]{2,1,0:T(8,128)(2,1)S(1)}, u32[]{:S(2)}, u32[]{:S(2)}) %all-to-all-start) | async-done | bytes 262176 | tf_op jit(solution)/shard_map/all_to_all | solution.py:452
  90.6 3.6 %all-to-all-start.1 = ((bf16[8,32,512]{2,1,0:T(8,128)(2,1)}), bf16[8,32,512]{2,1,0:T(8,128)(2,1)S(1)}, u32[]{:S(2)}, u32[]{:S(2)}) async-start(bf16[8,32,512]{2,1,0:T(8,128)(2,1)} %bitcast.30), calls=%async_computation.1 | async-start | bytes 524288 | tf_op jit(solution)/shard_map/all_to_all | solution.py:452
  96.5 5.6 %collective-permute-done.19.refs_1_ = bf16[32,4096]{1,0:T(8,128)(2,1)S(1)} collective-permute-done((bf16[32,4096]{1,0:T(8,128)(2,1)S(1)}, bf16[32,4096]{1,0:T(8,128)(2,1)S(1)}, u32[]{:S(2)}, u32[]{:S(2)}) %collective-permute-start.19) | collective-permute-done | bytes 262176 | tf_op jit(solution)/shard_map/ppermute | solution.py:24
  103.6 16.7 %experts.2 = (bf16[64,4096]{1,0:T(8,128)(2,1)S(1)}, bf16[64,4096]{1,0:T(8,128)(2,1)S(1)}) custom-call(bf16[32,4096]{1,0:T(8,128)(2,1)S(1)} %normed_rows.2.refs_0_, bf16[32,4096]{1,0:T(8,128)(2,1)S(1)} %collective-permute-done.19.refs_1_, bf16[32,4096]{1,0:T(8,128)(2,1)S(1)} %collective-permute-done.20.refs_2_, ...), custom_call_target="tpu_custom_call" | custom-call | flops 5033164800 | bytes 39321600 | tf_op jit(solution)/shard_map/experts/pallas_call | solution.py:268
  122.6 6.7 %collective-permute-done.24.refs_1_ = bf16[32,4096]{1,0:T(8,128)(2,1)S(1)} collective-permute-done((bf16[32,4096]{1,0:T(8,128)(2,1)S(1)}, bf16[32,4096]{1,0:T(8,128)(2,1)S(1)}, u32[]{:S(2)}, u32[]{:S(2)}) %collective-permute-start.24) | collective-permute-done | bytes 262176 | tf_op jit(solution)/shard_map/ppermute | solution.py:24
  130.8 16.7 %experts.3 = (bf16[64,4096]{1,0:T(8,128)(2,1)S(1)}, bf16[64,4096]{1,0:T(8,128)(2,1)S(1)}) custom-call(bf16[32,4096]{1,0:T(8,128)(2,1)S(1)} %normed_rows.3.refs_0_, bf16[32,4096]{1,0:T(8,128)(2,1)S(1)} %collective-permute-done.24.refs_1_, bf16[32,4096]{1,0:T(8,128)(2,1)S(1)} %collective-permute-done.25.refs_2_, ...), custom_call_target="tpu_custom_call" | custom-call | flops 5033164800 | bytes 39321600 | tf_op jit(solution)/shard_map/experts/pallas_call | solution.py:268
  151.2 6.1 %collective-permute-done.23 = bf16[32,4096]{1,0:T(8,128)(2,1)S(1)} collective-permute-done((bf16[32,4096]{1,0:T(8,128)(2,1)S(1)}, bf16[32,4096]{1,0:T(8,128)(2,1)S(1)}, u32[]{:S(2)}, u32[]{:S(2)}) %collective-permute-start.23) | collective-permute-done | bytes 262176 | tf_op jit(solution)/shard_map/ppermute | solution.py:24
  158.2 5.7 %all-to-all-start.2 = ((bf16[8,32,512]{2,1,0:T(8,128)(2,1)}), bf16[8,32,512]{2,1,0:T(8,128)(2,1)S(1)}, u32[]{:S(2)}, u32[]{:S(2)}) async-start(bf16[8,32,512]{2,1,0:T(8,128)(2,1)} %bitcast.119), calls=%async_computation.2 | async-start | bytes 524288 | tf_op jit(solution)/shard_map/all_to_all | solution.py:452
  164.7 7.4 %all-to-all-done.2 = bf16[8,32,512]{2,1,0:T(8,128)(2,1)S(1)} async-done(((bf16[8,32,512]{2,1,0:T(8,128)(2,1)}), bf16[8,32,512]{2,1,0:T(8,128)(2,1)S(1)}, u32[]{:S(2)}, u32[]{:S(2)}) %all-to-all-start.2) | async-done | bytes 262176 | tf_op jit(solution)/shard_map/all_to_all | solution.py:452
  172.1 3.4 %all-to-all-start.3 = ((bf16[8,32,512]{2,1,0:T(8,128)(2,1)}), bf16[8,32,512]{2,1,0:T(8,128)(2,1)S(1)}, u32[]{:S(2)}, u32[]{:S(2)}) async-start(bf16[8,32,512]{2,1,0:T(8,128)(2,1)} %bitcast.117), calls=%async_computation.3 | async-start | bytes 524288 | tf_op jit(solution)/shard_map/all_to_all | solution.py:452
  175.7 8.1 %all-to-all-done.3 = bf16[8,32,512]{2,1,0:T(8,128)(2,1)S(1)} async-done(((bf16[8,32,512]{2,1,0:T(8,128)(2,1)}), bf16[8,32,512]{2,1,0:T(8,128)(2,1)S(1)}, u32[]{:S(2)}, u32[]{:S(2)}) %all-to-all-start.3) | async-done | bytes 262176 | tf_op jit(solution)/shard_map/all_to_all | solution.py:452
  (130 shorter events, 48.6 us)
Async XLA Ops:
  0.0 20.3 %collective-permute-start = (bf16[128,512]{1,0:T(8,128)(2,1)}, bf16[128,512]{1,0:T(8,128)(2,1)S(1)}, u32[]{:S(2)}, u32[]{:S(2)}) collective-permute-start(bf16[128,512]{1,0:T(8,128)(2,1)} %refs_5_.3), channel_id=1, source_target_pairs={{0,4},{4,0},{8,12},{12,8},{16,20},{20,16},{24,28},{28,24},{1,5},{5... | collective-permute-start | bytes 393224 | tf_op jit(solution)/shard_map/ppermute | solution.py:24
  3.0 7.0 %collective-permute-start.1 = (bf16[128,512]{1,0:T(8,128)(2,1)}, bf16[128,512]{1,0:T(8,128)(2,1)S(1)}, u32[]{:S(2)}, u32[]{:S(2)}) collective-permute-start(bf16[128,512]{1,0:T(8,128)(2,1)} %refs_5_.3), channel_id=1, source_target_pairs={{0,8},{4,12},{8,0},{12,4},{16,24},{20,28},{24,16},{28,20},{1,9},{5... | collective-permute-start | bytes 393224 | tf_op jit(solution)/shard_map/ppermute | solution.py:24
  4.5 12.9 %collective-permute-start.3 = (bf16[128,512]{1,0:T(8,128)(2,1)}, bf16[128,512]{1,0:T(8,128)(2,1)S(1)}, u32[]{:S(2)}, u32[]{:S(2)}) collective-permute-start(bf16[128,512]{1,0:T(8,128)(2,1)} %refs_5_.3), channel_id=1, source_target_pairs={{0,16},{4,20},{8,24},{12,28},{16,0},{20,4},{24,8},{28,12},{1,17},{... | collective-permute-start | bytes 393224 | tf_op jit(solution)/shard_map/ppermute | solution.py:24
  7.1 10.8 %collective-permute-start.5 = (bf16[128,512]{1,0:T(8,128)(2,1)}, bf16[128,512]{1,0:T(8,128)(2,1)S(1)}, u32[]{:S(2)}, u32[]{:S(2)}) collective-permute-start(bf16[128,512]{1,0:T(8,128)(2,1)} %refs_5_.3), channel_id=1, source_target_pairs={{0,24},{4,28},{8,16},{12,20},{16,8},{20,12},{24,0},{28,4},{1,25},{... | collective-permute-start | bytes 393224 | tf_op jit(solution)/shard_map/ppermute | solution.py:24
  10.0 10.3 %collective-permute-start.2 = (bf16[128,512]{1,0:T(8,128)(2,1)S(1)}, bf16[128,512]{1,0:T(8,128)(2,1)S(1)}, u32[]{:S(2)}, u32[]{:S(2)}) collective-permute-start(bf16[128,512]{1,0:T(8,128)(2,1)S(1)} %collective-permute-done.1.refs_8_.refs_7_), channel_id=1, source_target_pairs={{0,4},{4,0},{8,12},{12,8},{16,20},{20,16},{24,28},{28,24},{1,5},{5... | collective-permute-start | bytes 393224 | tf_op jit(solution)/shard_map/ppermute | solution.py:24
  35.2 6.8 %collective-permute-start.10 = (bf16[2,128,128]{2,1,0:T(8,128)(2,1)S(1)}, bf16[2,128,128]{2,1,0:T(8,128)(2,1)S(1)}, u32[]{:S(2)}, u32[]{:S(2)}) collective-permute-start(bf16[2,128,128]{2,1,0:T(8,128)(2,1)S(1)} %get-tuple-element.44), channel_id=1, source_target_pairs={{0,24},{4,28},{8,16},{12,20},{16,8},{20,12},{24,0},{28,4},{1,25},{... | collective-permute-start | bytes 196616 | tf_op jit(solution)/shard_map/ppermute | solution.py:24
  54.2 9.2 %collective-permute-start.15 = (bf16[4,64,512]{2,1,0:T(8,128)(2,1)S(1)}, bf16[4,64,512]{2,1,0:T(8,128)(2,1)S(1)}, u32[]{:S(2)}, u32[]{:S(2)}) collective-permute-start(bf16[4,64,512]{2,1,0:T(8,128)(2,1)S(1)} %get-tuple-element.27), channel_id=1, source_target_pairs={{0,4},{4,0},{8,12},{12,8},{16,20},{20,16},{24,28},{28,24},{1,5},{5... | collective-permute-start | bytes 786440 | tf_op jit(solution)/shard_map/ppermute | solution.py:24
  55.0 13.4 %collective-permute-start.11 = (bf16[4,64,512]{2,1,0:T(8,128)(2,1)S(1)}, bf16[4,64,512]{2,1,0:T(8,128)(2,1)S(1)}, u32[]{:S(2)}, u32[]{:S(2)}) collective-permute-start(bf16[4,64,512]{2,1,0:T(8,128)(2,1)S(1)} %get-tuple-element.25), channel_id=1, source_target_pairs={{0,4},{4,0},{8,12},{12,8},{16,20},{20,16},{24,28},{28,24},{1,5},{5... | collective-permute-start | bytes 786440 | tf_op jit(solution)/shard_map/ppermute | solution.py:24
  63.5 7.1 %collective-permute-start.18 = (bf16[64,512]{1,0:T(8,128)(2,1)S(1)}, bf16[64,512]{1,0:T(8,128)(2,1)S(1)}, u32[]{:S(2)}, u32[]{:S(2)}) collective-permute-start(bf16[64,512]{1,0:T(8,128)(2,1)S(1)} %get-tuple-element.41), channel_id=1, source_target_pairs={{0,24},{4,28},{8,16},{12,20},{16,8},{20,12},{24,0},{28,4},{1,25},{... | collective-permute-start | bytes 196616 | tf_op jit(solution)/shard_map/ppermute | solution.py:24
  65.3 7.6 %collective-permute-start.17 = (bf16[64,512]{1,0:T(8,128)(2,1)S(1)}, bf16[64,512]{1,0:T(8,128)(2,1)S(1)}, u32[]{:S(2)}, u32[]{:S(2)}) collective-permute-start(bf16[64,512]{1,0:T(8,128)(2,1)S(1)} %get-tuple-element.42), channel_id=1, source_target_pairs={{0,16},{4,20},{8,24},{12,28},{16,0},{20,4},{24,8},{28,12},{1,17},{... | collective-permute-start | bytes 196616 | tf_op jit(solution)/shard_map/ppermute | solution.py:24
  65.6 7.4 %collective-permute-start.16 = (bf16[64,512]{1,0:T(8,128)(2,1)S(1)}, bf16[64,512]{1,0:T(8,128)(2,1)S(1)}, u32[]{:S(2)}, u32[]{:S(2)}) collective-permute-start(bf16[64,512]{1,0:T(8,128)(2,1)S(1)} %get-tuple-element.40), channel_id=1, source_target_pairs={{0,8},{4,12},{8,0},{12,4},{16,24},{20,28},{24,16},{28,20},{1,9},{5... | collective-permute-start | bytes 196616 | tf_op jit(solution)/shard_map/ppermute | solution.py:24
  70.3 7.1 %collective-permute-start.13 = (bf16[64,512]{1,0:T(8,128)(2,1)S(1)}, bf16[64,512]{1,0:T(8,128)(2,1)S(1)}, u32[]{:S(2)}, u32[]{:S(2)}) collective-permute-start(bf16[64,512]{1,0:T(8,128)(2,1)S(1)} %get-tuple-element.39), channel_id=1, source_target_pairs={{0,16},{4,20},{8,24},{12,28},{16,0},{20,4},{24,8},{28,12},{1,17},{... | collective-permute-start | bytes 196616 | tf_op jit(solution)/shard_map/ppermute | solution.py:24
  70.6 6.8 %collective-permute-start.12 = (bf16[64,512]{1,0:T(8,128)(2,1)S(1)}, bf16[64,512]{1,0:T(8,128)(2,1)S(1)}, u32[]{:S(2)}, u32[]{:S(2)}) collective-permute-start(bf16[64,512]{1,0:T(8,128)(2,1)S(1)} %get-tuple-element.37), channel_id=1, source_target_pairs={{0,8},{4,12},{8,0},{12,4},{16,24},{20,28},{24,16},{28,20},{1,9},{5... | collective-permute-start | bytes 196616 | tf_op jit(solution)/shard_map/ppermute | solution.py:24
  78.4 12.2 %all-to-all-start = ((bf16[8,32,512]{2,1,0:T(8,128)(2,1)}), bf16[8,32,512]{2,1,0:T(8,128)(2,1)S(1)}, u32[]{:S(2)}, u32[]{:S(2)}) async-start(bf16[8,32,512]{2,1,0:T(8,128)(2,1)} %bitcast.27), calls=%async_computation | async-start | bytes 524288 | tf_op jit(solution)/shard_map/all_to_all | solution.py:452
  90.6 12.2 %all-to-all-start.1 = ((bf16[8,32,512]{2,1,0:T(8,128)(2,1)}), bf16[8,32,512]{2,1,0:T(8,128)(2,1)S(1)}, u32[]{:S(2)}, u32[]{:S(2)}) async-start(bf16[8,32,512]{2,1,0:T(8,128)(2,1)} %bitcast.30), calls=%async_computation.1 | async-start | bytes 524288 | tf_op jit(solution)/shard_map/all_to_all | solution.py:452
  94.5 7.5 %collective-permute-start.19 = (bf16[32,4096]{1,0:T(8,128)(2,1)S(1)}, bf16[32,4096]{1,0:T(8,128)(2,1)S(1)}, u32[]{:S(2)}, u32[]{:S(2)}) collective-permute-start(bf16[32,4096]{1,0:T(8,128)(2,1)S(1)} %normed_rows.2.refs_0_), channel_id=1, source_target_pairs={{0,2},{1,3},{2,0},{3,1},{4,6},{5,7},{6,4},{7,5},{8,10},{9,11},{10,... | collective-permute-start | bytes 786440 | tf_op jit(solution)/shard_map/ppermute | solution.py:24
  96.4 6.7 %collective-permute-start.20 = (bf16[32,4096]{1,0:T(8,128)(2,1)S(1)}, bf16[32,4096]{1,0:T(8,128)(2,1)S(1)}, u32[]{:S(2)}, u32[]{:S(2)}) collective-permute-start(bf16[32,4096]{1,0:T(8,128)(2,1)S(1)} %normed_rows.2.refs_0_), channel_id=1, source_target_pairs={{0,1},{1,0},{2,3},{3,2},{4,5},{5,4},{6,7},{7,6},{8,9},{9,8},{10,11... | collective-permute-start | bytes 786440 | tf_op jit(solution)/shard_map/ppermute | solution.py:24
  120.3 9.0 %collective-permute-start.22 = (bf16[64,4096]{1,0:T(8,128)(2,1)S(1)}, bf16[64,4096]{1,0:T(8,128)(2,1)S(1)}, u32[]{:S(2)}, u32[]{:S(2)}) collective-permute-start(bf16[64,4096]{1,0:T(8,128)(2,1)S(1)} %get-tuple-element.31), channel_id=1, source_target_pairs={{0,1},{1,0},{2,3},{3,2},{4,5},{5,4},{6,7},{7,6},{8,9},{9,8},{10,11... | collective-permute-start | bytes 1572872 | tf_op jit(solution)/shard_map/ppermute | solution.py:24
  120.7 8.6 %collective-permute-start.24 = (bf16[32,4096]{1,0:T(8,128)(2,1)S(1)}, bf16[32,4096]{1,0:T(8,128)(2,1)S(1)}, u32[]{:S(2)}, u32[]{:S(2)}) collective-permute-start(bf16[32,4096]{1,0:T(8,128)(2,1)S(1)} %normed_rows.3.refs_0_), channel_id=1, source_target_pairs={{0,2},{1,3},{2,0},{3,1},{4,6},{5,7},{6,4},{7,5},{8,10},{9,11},{10,... | collective-permute-start | bytes 786440 | tf_op jit(solution)/shard_map/ppermute | solution.py:24
  122.4 7.0 %collective-permute-start.25 = (bf16[32,4096]{1,0:T(8,128)(2,1)S(1)}, bf16[32,4096]{1,0:T(8,128)(2,1)S(1)}, u32[]{:S(2)}, u32[]{:S(2)}) collective-permute-start(bf16[32,4096]{1,0:T(8,128)(2,1)S(1)} %normed_rows.3.refs_0_), channel_id=1, source_target_pairs={{0,1},{1,0},{2,3},{3,2},{4,5},{5,4},{6,7},{7,6},{8,9},{9,8},{10,11... | collective-permute-start | bytes 786440 | tf_op jit(solution)/shard_map/ppermute | solution.py:24
  148.1 9.2 %collective-permute-start.23 = (bf16[32,4096]{1,0:T(8,128)(2,1)S(1)}, bf16[32,4096]{1,0:T(8,128)(2,1)S(1)}, u32[]{:S(2)}, u32[]{:S(2)}) collective-permute-start(bf16[32,4096]{1,0:T(8,128)(2,1)S(1)} %slice.257), channel_id=1, source_target_pairs={{0,2},{1,3},{2,0},{3,1},{4,6},{5,7},{6,4},{7,5},{8,10},{9,11},{10,... | collective-permute-start | bytes 786440 | tf_op jit(solution)/shard_map/ppermute | solution.py:24
  149.8 14.0 %collective-permute-start.28 = (bf16[32,4096]{1,0:T(8,128)(2,1)S(1)}, bf16[32,4096]{1,0:T(8,128)(2,1)S(1)}, u32[]{:S(2)}, u32[]{:S(2)}) collective-permute-start(bf16[32,4096]{1,0:T(8,128)(2,1)S(1)} %slice.256), channel_id=1, source_target_pairs={{0,2},{1,3},{2,0},{3,1},{4,6},{5,7},{6,4},{7,5},{8,10},{9,11},{10,... | collective-permute-start | bytes 786440 | tf_op jit(solution)/shard_map/ppermute | solution.py:24
  158.2 13.9 %all-to-all-start.2 = ((bf16[8,32,512]{2,1,0:T(8,128)(2,1)}), bf16[8,32,512]{2,1,0:T(8,128)(2,1)S(1)}, u32[]{:S(2)}, u32[]{:S(2)}) async-start(bf16[8,32,512]{2,1,0:T(8,128)(2,1)} %bitcast.119), calls=%async_computation.2 | async-start | bytes 524288 | tf_op jit(solution)/shard_map/all_to_all | solution.py:452
  172.1 11.8 %all-to-all-start.3 = ((bf16[8,32,512]{2,1,0:T(8,128)(2,1)}), bf16[8,32,512]{2,1,0:T(8,128)(2,1)S(1)}, u32[]{:S(2)}, u32[]{:S(2)}) async-start(bf16[8,32,512]{2,1,0:T(8,128)(2,1)} %bitcast.117), calls=%async_computation.3 | async-start | bytes 524288 | tf_op jit(solution)/shard_map/all_to_all | solution.py:452
  (23 other events, 193.3 us)
where the time goes:
time: 186 us; the launch traced here: 185 us
  waiting for transfers between devices  73.2 us (39%)
  starting transfers between devices  48.9 us (26%)
  Pallas kernels  38.4 us (21%)
  local copies, waits for them, and re-layouts  10.1 us (5%)
  blocking collectives  5.78 us (3%)
  matrix products  4.64 us (2%)
  other arithmetic  3.31 us (2%)
    ppermute x29, waiting for transfers between devices, swap(): return lax.ppermute(values, axis, [(i, i ^ distance) for i in range(count)])  49.3 us
    pallas_call x2, Pallas kernels, expert_partial(): pl.pallas_call(kernel, grid=(parts, steps), in_specs=[pl.BlockSpec(piece....  33.4 us
    ppermute x29, starting transfers between devices, swap(): return lax.ppermute(values, axis, [(i, i ^ distance) for i in range(count)])  32.8 us
    all_to_all x4, waiting for transfers between devices, exchange(): lax.all_to_all(blocks_of, 'wide', split_axis=0, concat_axis=0, tiled=True)  24 us
    all_to_all x4, starting transfers between devices, exchange(): lax.all_to_all(blocks_of, 'wide', split_axis=0, concat_axis=0, tiled=True)  16.1 us
    unnamed x29, local copies, waits for them, and re-layouts  6.36 us
    all_gather x1, blocking collectives, body(): span = lax.all_gather(fresh, 'narrow', axis=1, tiled=True)  5.78 us
  transfers between devices with their start and end apart: 33, of which 19 were waited for; matrix products, arithmetic and copies ran while one was open for 5% of the time, Pallas kernels for 1%

commit v1 on v0

--- a/solution.py
+++ b/solution.py
@@ -1,6 +1,5 @@
 import jax
 import jax.numpy as jnp
-import numpy as np
 from jax import lax
 from jax.experimental import pallas as pl
 from jax.experimental.pallas import tpu as pltpu
@@ -45,10 +44,9 @@
         gathered = lax.all_gather(values, axis, axis=0)
         return [gathered[i] for i in range(count)]
     held = {0: values}
-    for distance in range(2, count, 2):
-        held[distance] = swap(values, axis, distance)
-    for distance in range(1, count, 2):
-        held[distance] = swap(held[distance - 1], axis, 1)
+    for distance in sorted(range(1, count), key=lambda d: (bin(d).count("1"), -d)):
+        last = distance & -distance
+        held[distance] = swap(held[distance - last], axis, last)
     return [held[distance] for distance in range(count)]
 
 
@@ -80,6 +78,28 @@
 VMEM_SPEC = pl.BlockSpec(memory_space=pltpu.VMEM)
 
 
+def load(*arrays):
+    def kernel(*refs):
+        count = len(arrays)
+        copies = [
+            pltpu.make_async_copy(refs[i], refs[count + i], refs[2 * count].at[i])
+            for i in range(count)
+        ]
+        for copy in copies:
+            copy.start()
+        for copy in copies:
+            copy.wait()
+
+    return pl.pallas_call(
+        kernel,
+        in_specs=[pl.BlockSpec(memory_space=pltpu.HBM)] * len(arrays),
+        out_specs=[VMEM_SPEC] * len(arrays),
+        out_shape=[jax.ShapeDtypeStruct(a.shape, a.dtype) for a in arrays],
+        scratch_shapes=[pltpu.SemaphoreType.DMA((len(arrays),))],
+        compiler_params=pltpu.CompilerParams(vmem_limit_bytes=SMALL_VMEM),
+    )(*arrays)
+
+
 def row_statistics(blocks, features):
     rows = blocks[0].shape[0]
     total = jnp.zeros((rows, 1), jnp.float32)
@@ -108,7 +128,7 @@
         average, scale = row_statistics(block_refs, share * count)
         mean_ref[...] = average
         scale_ref[...] = scale
-        n = ((own_ref[...].astype(f32) - average) * scale * gain_ref[...]).astype(bf16)
+        n = ((own_ref[...].astype(f32) - average) * scale * gain_ref[group_ref[count]]).astype(bf16)
         for which, ref in enumerate((k_ref, v_ref)):
             term = jnp.dot(n, ref[...], preferred_element_type=f32).astype(bf16)
             for c in range(columns):
@@ -164,19 +184,61 @@
         scratch_shapes=[pltpu.VMEM((rows, width), f32)],
         compiler_params=pltpu.CompilerParams(vmem_limit_bytes=SMALL_VMEM),
         name="queries",
-    )(order, average, scale, gain.reshape(count, 1, share), query_weight, *blocks)
-
-
-def mix_terms(attended, out_weight, order, chunks):
+    )(order, average, scale, gain, query_weight, *blocks)
+
+
+def mix_terms(queries, pieces, cache_key, cache_value, out_weight, order, place, chunks):
     f32, bf16 = jnp.float32, jnp.bfloat16
-    rows = attended.shape[0]
+    rows, inner = queries.shape
+    _, head_size = cache_key.shape[1:]
+    kv_here = pieces[0][1].shape[2] // head_size
+    per_group = inner // head_size // kv_here
     count = order.shape[0]
     share = out_weight.shape[1] // count
     far, near = split_order("wide")
     half, chunk = count // 2, rows // chunks
-
-    def kernel(order_ref, a_ref, w_ref, *out_refs):
-        a = a_ref[...]
+    by_rows = (((1,), (1,)), ((), ()))
+    distances = [distance for distance, _ in pieces]
+
+    def kernel(order_ref, place_ref, q_ref, ck_ref, cv_ref, w_ref, *refs):
+        piece_refs, out_refs, attended = refs[: len(pieces)], refs[len(pieces) : -1], refs[-1]
+        here = place_ref[1]
+        shape = (per_group * rows, rows)
+        causal = lax.broadcasted_iota(jnp.int32, shape, 1) <= lax.rem(
+            lax.broadcasted_iota(jnp.int32, shape, 0), rows
+        )
+        for g in range(kv_here):
+            first = g * per_group
+            columns = slice(g * head_size, (g + 1) * head_size)
+            q = jnp.concatenate(
+                [
+                    q_ref[:, (first + h) * head_size : (first + h + 1) * head_size]
+                    for h in range(per_group)
+                ]
+            )
+            score = lambda keys: lax.dot_general(
+                q, keys, by_rows, preferred_element_type=f32
+            ) * (head_size ** (-0.5))
+            scores = [score(ck_ref[place_ref[0] + g])]
+            values = [cv_ref[place_ref[0] + g]]
+            for distance, ref in zip(distances, piece_refs):
+                allowed = causal if distance == 0 else (here ^ distance) < here
+                scores.append(jnp.where(allowed, score(ref[0, :, columns]), -1e30))
+                values.append(ref[1, :, columns])
+            highest = scores[0].max(axis=1, keepdims=True)
+            for s in scores[1:]:
+                highest = jnp.maximum(highest, s.max(axis=1, keepdims=True))
+            weights = [jnp.exp(s - highest) for s in scores]
+            total = sum(w.sum(axis=1, keepdims=True) for w in weights)
+            mixed = sum(
+                jnp.dot((w / total).astype(bf16), v, preferred_element_type=f32)
+                for w, v in zip(weights, values)
+            ).astype(bf16)
+            for h in range(per_group):
+                attended[:, (first + h) * head_size : (first + h + 1) * head_size] = mixed[
+                    h * rows : (h + 1) * rows
+                ]
+        a = attended[...]
         for side, positions in enumerate((far, near)):
             for i, position in enumerate(positions):
                 at = pl.multiple_of(order_ref[position] * share, share)
@@ -186,12 +248,13 @@
 
     outs = pl.pallas_call(
         kernel,
-        in_specs=[SMEM_SPEC] + [VMEM_SPEC] * 2,
+        in_specs=[SMEM_SPEC] * 2 + [VMEM_SPEC] * (4 + len(pieces)),
         out_specs=[VMEM_SPEC] * (2 * chunks),
         out_shape=[jax.ShapeDtypeStruct((half, chunk, share), bf16)] * (2 * chunks),
+        scratch_shapes=[pltpu.VMEM((rows, inner), bf16)],
         compiler_params=pltpu.CompilerParams(vmem_limit_bytes=SMALL_VMEM),
         name="mix_terms",
-    )(order, attended, out_weight)
+    )(order, place, queries, cache_key, cache_value, out_weight, *[p for _, p in pieces])
     return outs[:chunks], outs[chunks:]
 
 
@@ -200,26 +263,44 @@
     features = owners * share
 
     def kernel(x_ref, g_ref, out_ref):
-        total = jnp.zeros((rows, 1), jnp.float32)
-        for o in range(owners):
-            total += jnp.sum(x_ref[o].astype(jnp.float32), axis=1, keepdims=True)
-        average = total / features
-        square = jnp.zeros((rows, 1), jnp.float32)
-        for o in range(owners):
-            centered = x_ref[o].astype(jnp.float32) - average
-            square += jnp.sum(centered * centered, axis=1, keepdims=True)
-        scale = lax.rsqrt(square / features + epsilon)
-        for o in range(owners):
+        blocks = [x_ref.at[o] for o in range(owners)]
+        average, scale = row_statistics(blocks, features)
+        for o, block in enumerate(blocks):
             at = slice(o * share, (o + 1) * share)
-            centered = x_ref[o].astype(jnp.float32) - average
+            centered = block[...].astype(jnp.float32) - average
             out_ref[:, at] = (centered * scale * g_ref[:, at]).astype(jnp.bfloat16)
 
     return pl.pallas_call(
         kernel,
+        in_specs=[VMEM_SPEC] * 2,
+        out_specs=VMEM_SPEC,
         out_shape=jax.ShapeDtypeStruct((rows, features), jnp.bfloat16),
         compiler_params=pltpu.CompilerParams(vmem_limit_bytes=SMALL_VMEM),
         name="normed_rows",
-    )(got, gain.reshape(1, -1))
+    )(got, gain)
+
+
+def cut_rows(rows, weights, count):
+    share = rows[0].shape[1] // count
+    total = sum(r.shape[0] for r in rows)
+
+    def kernel(*refs):
+        out_ref = refs[-1]
+        at = 0
+        for x_ref, w_ref in zip(refs[: len(rows)], refs[len(rows) : -1]):
+            for o in range(count):
+                block = x_ref[:, o * share : (o + 1) * share] * w_ref[...]
+                out_ref[o, at : at + x_ref.shape[0]] = block.astype(jnp.bfloat16)
+            at += x_ref.shape[0]
+
+    return pl.pallas_call(
+        kernel,
+        in_specs=[VMEM_SPEC] * (2 * len(rows)),
+        out_specs=VMEM_SPEC,
+        out_shape=jax.ShapeDtypeStruct((count, total, share), jnp.bfloat16),
+        compiler_params=pltpu.CompilerParams(vmem_limit_bytes=SMALL_VMEM),
+        name="cut_rows",
+    )(*rows, *weights)
 
 
 def expert_partial(pieces, gate_weight, up_weight, down_weight, first, parts):
@@ -294,28 +375,6 @@
     earlier = jnp.cumsum(onehot, axis=1) - onehot
     position = jnp.sum(earlier * onehot, axis=2)
     return (flat_ids * capacity + position).reshape(routing.shape)
-
-
-def attend(queries, all_keys, all_values, first_row, context):
-    row_count, heads_here, head_size = queries.shape
-    kv_here = all_keys.shape[0]
-    grouped = queries.reshape(row_count, kv_here, heads_here // kv_here, head_size)
-    scale_factor = head_size ** (-0.5)
-    scores = (
-        jnp.einsum("rgqd,gkd->gqrk", grouped, all_keys, preferred_element_type=jnp.float32)
-        * scale_factor
-    )
-    row_ids = first_row + jnp.arange(row_count, dtype=jnp.int32)
-    key_ids = jnp.arange(all_keys.shape[1], dtype=jnp.int32) - context
-    allowed = key_ids[None, :] <= row_ids[:, None]
-    scores = jnp.where(allowed[None, None], scores, -1e30)
-    highest = jnp.max(scores, axis=3, keepdims=True)
-    weights = jnp.exp(scores - highest)
-    weights = (weights / jnp.sum(weights, axis=3, keepdims=True)).astype(jnp.bfloat16)
-    mixed = jnp.einsum(
-        "gqrk,gkd->rgqd", weights, all_values, preferred_element_type=jnp.float32
-    ).astype(jnp.bfloat16)
-    return mixed.reshape(row_count, heads_here, head_size)
 
 
 def gather_pieces(rows):
@@ -367,7 +426,7 @@
     narrow_index = lax.axis_index("narrow")
     narrow_count = lax.axis_size("narrow")
     row_count, feature_share = hidden.shape
-    kv_total, context, head_size = cache_key.shape
+    kv_total, _, head_size = cache_key.shape
     heads_here = query_weight.shape[1] // head_size
     share = heads_here * wide_count // kv_total
     kv_here = max(heads_here // share, 1)
@@ -378,75 +437,65 @@
     experts_here = max(slots_here // SPLIT, 1)
     parts_here = slots_here // experts_here
     blocks = row_count // TOK_BLOCK
-    routing = expert_ids.reshape(blocks, TOK_BLOCK, 2)
-    target = slot_targets(routing, experts, CAPD).reshape(row_count, 2)
-    token_block = np.arange(row_count) // TOK_BLOCK
-    dest_expert = (np.arange(wide_count)[:, None] * slots_here) // SPLIT + np.arange(experts_here)
-    slot_of_row = np.broadcast_to(
-        dest_expert[:, :, None, None] * CAPD + np.arange(CAPD),
-        (wide_count, experts_here, blocks, CAPD),
-    ).reshape(-1)
-    block_of_row = np.broadcast_to(
-        np.arange(blocks)[:, None], (wide_count, experts_here, blocks, CAPD)
-    ).reshape(-1)
-    row_slot = jnp.asarray(slot_of_row, jnp.int32)[:, None]
-    same_block = jnp.asarray(block_of_row, jnp.int32)[:, None] == jnp.asarray(
-        token_block, jnp.int32
-    )
-    first_pick = (row_slot == target[:, 0][None, :]) & same_block
-    second_pick = (row_slot == target[:, 1][None, :]) & same_block
-    picks = (first_pick | second_pick).astype(bf16)
-
     order = owners_by_distance("wide")
     gathered = gather_blocks(hidden, "wide")
-    own_gain = lax.dynamic_slice_in_dim(attn_gain, wide_index * feature_share, feature_share, 0)
+    gain_blocks = attn_gain.reshape(wide_count, 1, feature_share)
+    key_weight, value_weight, gain_blocks, own_block = load(
+        key_weight, value_weight, gain_blocks, hidden
+    )
+    if travels_directly("wide"):
+        gathered[0] = own_block
     kv_width = kv_here * head_size
     group_of = jnp.arange(wide_count, dtype=jnp.int32) * heads_here // share
     far_kv, near_kv, average, scale = key_value_terms(
         gathered,
-        hidden,
-        own_gain.reshape(1, -1),
+        own_block,
+        gain_blocks,
         key_weight,
         value_weight,
         order,
-        group_of,
+        jnp.append(group_of, wide_index).astype(jnp.int32),
         head_size,
         kv_width,
     )
+    cache_key, cache_value, mlp_gain_row = load(cache_key, cache_value, mlp_gain.reshape(1, -1))
     fresh = sum_blocks(far_kv, near_kv, "wide").astype(bf16)
-    queries = query_rows(gathered, average, scale, attn_gain, query_weight, order)
-    span = lax.all_gather(fresh, "narrow", axis=1, tiled=True)
-    span = span.reshape(2, -1, kv_here, head_size).transpose(0, 2, 1, 3)
-    own_cache_key = lax.dynamic_slice_in_dim(cache_key, kv_start, kv_here, 0)
-    own_cache_value = lax.dynamic_slice_in_dim(cache_value, kv_start, kv_here, 0)
-    all_keys = jnp.concatenate([own_cache_key, span[0]], axis=1)
-    all_values = jnp.concatenate([own_cache_value, span[1]], axis=1)
-    attended = attend(
-        queries.reshape(row_count, heads_here, head_size),
-        all_keys,
-        all_values,
-        narrow_index * row_count,
-        context,
-    ).reshape(row_count, heads_here * head_size)
-    far_mix, near_mix = mix_terms(attended, out_weight, order, MIX_CHUNKS)
+    queries = query_rows(gathered, average, scale, gain_blocks, query_weight, order)
+    span = gather_pieces(fresh)
+    distances = sorted(range(narrow_count), key=lambda d: (d & 1, d))
+    far_mix, near_mix = mix_terms(
+        queries,
+        list(zip(distances, span)),
+        cache_key,
+        cache_value,
+        out_weight,
+        order,
+        jnp.stack([kv_start, narrow_index]).astype(jnp.int32),
+        MIX_CHUNKS,
+    )
+    expert_ids = after(expert_ids, far_mix[0])
+    routing = expert_ids.reshape(blocks, TOK_BLOCK, 2)
+    target = slot_targets(routing, experts, CAPD).reshape(row_count, 2)
+    token_block = jnp.arange(row_count, dtype=jnp.int32) // TOK_BLOCK
+    dest_expert = (jnp.arange(wide_count, dtype=jnp.int32) * slots_here // SPLIT)[:, None] + jnp.arange(
+        experts_here, dtype=jnp.int32
+    )
+    expert_rows = blocks * CAPD
+    in_expert = jnp.arange(expert_rows, dtype=jnp.int32)
+    row_slot = dest_expert[:, :, None, None] * CAPD + (in_expert % CAPD)[:, None]
+    same_block = (in_expert // CAPD)[:, None] == token_block
+    first_pick = (row_slot == target[:, 0]) & same_block
+    second_pick = (row_slot == target[:, 1]) & same_block
+    picks = lax.optimization_barrier((first_pick | second_pick).astype(bf16))
     mixed = [sum_blocks(far, near, "wide") for far, near in zip(far_mix, near_mix)]
     residual = (hidden.astype(f32) + jnp.concatenate(mixed)).astype(bf16)
 
-    expert_rows = blocks * CAPD
-    picks = picks.reshape(wide_count, experts_here, expert_rows, row_count)
-    first_pick = first_pick.astype(f32).reshape(wide_count, experts_here, expert_rows, row_count)
-    second_pick = second_pick.astype(f32).reshape(wide_count, experts_here, expert_rows, row_count)
-    mine = lambda values: lax.dynamic_index_in_dim(values, wide_index, 0, keepdims=False)
+    mine = lambda values: lax.dynamic_index_in_dim(
+        values.astype(f32), wide_index, 0, keepdims=False
+    )
     my_first, my_second = mine(first_pick), mine(second_pick)
     ids_onehot = (expert_ids[:, :, None] == jnp.arange(experts, dtype=jnp.int32)).astype(f32)
     ids_diff = ids_onehot[:, 0] - ids_onehot[:, 1]
-
-    def choose(e):
-        return jnp.dot(
-            picks[:, e].reshape(wide_count * expert_rows, row_count),
-            residual,
-            preferred_element_type=f32,
-        ).astype(bf16)
 
     def exchange(blocks_of):
         return lax.all_to_all(blocks_of, "wide", split_axis=0, concat_axis=0, tiled=True)
@@ -457,34 +506,27 @@
         leading = jax.nn.sigmoid(jnp.sum(logits * ids, axis=1))
         return jnp.where(jnp.sum(my_first[e], axis=1) > 0, leading, 1.0 - leading)
 
-    def finish(e, own, other, distance):
+    def finish(own, other, distance):
         while True:
             own = own + swap(other, "narrow", distance).astype(f32)
             distance //= 2
             if distance < 2:
                 break
             own, other = split_rows(own)
-        weighted = (own * row_weights[e][:, None]).astype(bf16)
-        back = exchange(
-            weighted.reshape(expert_rows, wide_count, feature_share).transpose(1, 0, 2)
-        )
-        return lax.dot_general(
-            picks[:, e].reshape(wide_count * expert_rows, row_count),
-            back.reshape(-1, feature_share),
-            (((0,), (0,)), ((), ())),
-            preferred_element_type=f32,
-        )
+        return own
 
     gate_rows, up_rows = jnp.swapaxes(gate_weight, 1, 2), jnp.swapaxes(up_weight, 1, 2)
+    chosen = jnp.dot(
+        picks.transpose(1, 0, 2, 3).reshape(-1, row_count), residual, preferred_element_type=f32
+    ).astype(bf16)
+    chosen = chosen.reshape(experts_here, wide_count, expert_rows, feature_share)
     arrived = []
     for e in range(experts_here):
-        chosen = choose(e).reshape(wide_count, expert_rows, feature_share)
-        arrived.append(exchange(after(chosen, *arrived[-1:])))
-    normed_two = [normed_rows(got, mlp_gain) for got in arrived]
+        arrived.append(exchange(after(chosen[e], *arrived[-1:])))
+    normed_two = [normed_rows(got, mlp_gain_row) for got in arrived]
     row_weights = [weights_of(e, normed_two[e]) for e in range(experts_here)]
     pieces = [gather_pieces(rows) for rows in normed_two]
-    result = residual.astype(f32)
-    waiting = normed_two[1:2]
+    waiting = []
     sums = []
     for e in range(experts_here):
         tokens = [after(pieces[e][0], *waiting)] + pieces[e][1:]
@@ -494,9 +536,15 @@
         own, other = split_rows(start_narrow_sum(keep, far_rows))
         waiting = [other]
         sums.append((own, other))
-    for e in range(experts_here):
-        result = result + finish(e, *sums[e], narrow_count // 2)
-    return result.astype(bf16)
+    own_rows = [finish(*sums[e], narrow_count // 2) for e in range(experts_here)]
+    back = exchange(cut_rows(own_rows, [w[:, None] for w in row_weights], wide_count))
+    mixture = lax.dot_general(
+        picks.reshape(-1, row_count),
+        back.reshape(-1, feature_share),
+        (((0,), (0,)), ((), ())),
+        preferred_element_type=f32,
+    )
+    return (residual.astype(f32) + mixture).astype(bf16)
 
 
 def solution(mesh):

time: 186 us -> 185 us (level)
  blocking collectives: 5.78 us -> 18.8 us
  waiting for transfers between devices: 73.2 us -> 62 us
  starting transfers between devices: 48.9 us -> 42.6 us
  local copies, waits for them, and re-layouts: 10.1 us -> 14.8 us
  Pallas kernels: 38.4 us -> 40.3 us
    all_to_all x0 -> x1, blocking collectives: none -> 18.8 us  [exchange(): lax.all_to_all(blocks_of, 'wide', split_axis=0, concat_axis=0, tiled=True)]
    all_to_all x4 -> x2, waiting for transfers between devices: 24 us -> 8.31 us  [exchange(): lax.all_to_all(blocks_of, 'wide', split_axis=0, concat_axis=0, tiled=True)]
    all_to_all x4 -> x2, starting transfers between devices: 16.1 us -> 8.23 us  [exchange(): lax.all_to_all(blocks_of, 'wide', split_axis=0, concat_axis=0, tiled=True)]
    all_gather x1 -> x0, blocking collectives: 5.78 us -> none  [body(): span = lax.all_gather(fresh, 'narrow', axis=1, tiled=True)]
    unnamed x29 -> x22, local copies, waits for them, and re-layouts: 6.36 us -> 11.6 us
    ppermute x29 -> x32, waiting for transfers between devices: 49.3 us -> 53.7 us  [swap(): return lax.ppermute(values, axis, [(i, i ^ distance) for i in range(count)])]
    pallas_call x3 -> x6, Pallas kernels: 1.98 us -> 3.89 us  [the longest x1 2.55 us: mix_terms(): pl.pallas_call(kernel, in_specs=[SMEM_SPEC] * 2 + [VMEM_SPEC] * (4 + len(...]
    dot_general x6 -> x2, matrix products: 3.91 us -> 2.11 us  [the longest x1 1.19 us: body(): jnp.dot(picks.transpose(1, 0, 2, 3).reshape(-1, row_count), residual, pre...]
  transfers between devices with their start and end apart: 33 -> 34, of which waited for: 19 -> 19; matrix products, arithmetic and copies ran while one was open for 5% -> 3% of each run, Pallas kernels for 1% -> 10%
where the time goes in v1:
time: 185 us
  waiting for transfers between devices  62 us (34%)
  starting transfers between devices  42.6 us (23%)
  Pallas kernels  40.3 us (22%)
  blocking collectives  18.8 us (10%)
  local copies, waits for them, and re-layouts  14.8 us (8%)
  other arithmetic  3.06 us (2%)
  matrix products  2.84 us (2%)
    ppermute x32, waiting for transfers between devices, swap(): return lax.ppermute(values, axis, [(i, i ^ distance) for i in range(count)])  53.7 us
    ppermute x32, starting transfers between devices, swap(): return lax.ppermute(values, axis, [(i, i ^ distance) for i in range(count)])  34.4 us
    pallas_call x2, Pallas kernels, expert_partial(): pl.pallas_call(kernel, grid=(parts, steps), in_specs=[pl.BlockSpec(piece....  33.4 us
    all_to_all x1, blocking collectives, exchange(): lax.all_to_all(blocks_of, 'wide', split_axis=0, concat_axis=0, tiled=True)  18.8 us
    unnamed x22, local copies, waits for them, and re-layouts  11.6 us
    all_to_all x2, waiting for transfers between devices, exchange(): lax.all_to_all(blocks_of, 'wide', split_axis=0, concat_axis=0, tiled=True)  8.31 us
    all_to_all x2, starting transfers between devices, exchange(): lax.all_to_all(blocks_of, 'wide', split_axis=0, concat_axis=0, tiled=True)  8.23 us
  transfers between devices with their start and end apart: 34, of which 19 were waited for; matrix products, arithmetic and copies ran while one was open for 3% of the time, Pallas kernels for 10%

profile of v1, /device:TPU:0, one launch (start us, length us, event | category | flops | bytes accessed | tf_op | source)
XLA Modules:
  0.0 184.7 jit_solution(8480206822751437258)
XLA Ops:
  0.0 4.1 %collective-permute-start.3 = (bf16[128,512]{1,0:T(8,128)(2,1)}, bf16[128,512]{1,0:T(8,128)(2,1)S(1)}, u32[]{:S(2)}, u32[]{:S(2)}) collective-permute-start(bf16[128,512]{1,0:T(8,128)(2,1)} %refs_3_.1), channel_id=1, source_target_pairs={{0,16},{4,20},{8,24},{12,28},{16,0},{20,4},{24,8},{28,12},{1,17},{... | collective-permute-start | bytes 393224 | tf_op jit(solution)/shard_map/ppermute | solution.py:23
  7.1 3.5 %collective-permute-done.3.refs_10_.refs_9_ = bf16[128,512]{1,0:T(8,128)(2,1)S(1)} collective-permute-done((bf16[128,512]{1,0:T(8,128)(2,1)}, bf16[128,512]{1,0:T(8,128)(2,1)S(1)}, u32[]{:S(2)}, u32[]{:S(2)}) %collective-permute-start.3) | collective-permute-done | bytes 131104 | tf_op jit(solution)/shard_map/ppermute | solution.py:23
  13.6 2.0 %collective-permute-done.5.refs_12_.refs_11_ = bf16[128,512]{1,0:T(8,128)(2,1)S(1)} collective-permute-done((bf16[128,512]{1,0:T(8,128)(2,1)S(1)}, bf16[128,512]{1,0:T(8,128)(2,1)S(1)}, u32[]{:S(2)}, u32[]{:S(2)}) %collective-permute-start.5) | collective-permute-done | bytes 131104 | tf_op jit(solution)/shard_map/ppermute | solution.py:23
  25.5 5.6 %collective-permute-done.7 = bf16[4,2,128,128]{3,2,1,0:T(8,128)(2,1)S(1)} collective-permute-done((bf16[4,2,128,128]{3,2,1,0:T(8,128)(2,1)S(1)}, bf16[4,2,128,128]{3,2,1,0:T(8,128)(2,1)S(1)}, u32[]{:S(2)}, u32[]{:S(2)}) %collective-permute-start.7) | collective-permute-done | bytes 262176 | tf_op jit(solution)/shard_map/ppermute | solution.py:23
  31.2 3.3 %collective-permute-start.10 = (bf16[2,128,128]{2,1,0:T(8,128)(2,1)S(1)}, bf16[2,128,128]{2,1,0:T(8,128)(2,1)S(1)}, u32[]{:S(2)}, u32[]{:S(2)}) collective-permute-start(bf16[2,128,128]{2,1,0:T(8,128)(2,1)S(1)} %get-tuple-element.60), channel_id=1, source_target_pairs={{0,24},{4,28},{8,16},{12,20},{16,8},{20,12},{24,0},{28,4},{1,25},{... | collective-permute-start | bytes 196616 | tf_op jit(solution)/shard_map/ppermute | solution.py:23
  35.6 2.1 %collective-permute-done.10 = bf16[2,128,128]{2,1,0:T(8,128)(2,1)S(1)} collective-permute-done((bf16[2,128,128]{2,1,0:T(8,128)(2,1)S(1)}, bf16[2,128,128]{2,1,0:T(8,128)(2,1)S(1)}, u32[]{:S(2)}, u32[]{:S(2)}) %collective-permute-start.10) | collective-permute-done | bytes 65568 | tf_op jit(solution)/shard_map/ppermute | solution.py:23
  37.7 2.6 %collective-permute-done.9 = bf16[2,128,128]{2,1,0:T(8,128)(2,1)S(1)} collective-permute-done((bf16[2,128,128]{2,1,0:T(8,128)(2,1)S(1)}, bf16[2,128,128]{2,1,0:T(8,128)(2,1)S(1)}, u32[]{:S(2)}, u32[]{:S(2)}) %collective-permute-start.9) | collective-permute-done | bytes 65568 | tf_op jit(solution)/shard_map/ppermute | solution.py:23
  46.1 2.2 %copy-done.1 = bf16[4096,512]{1,0:T(8,128)(2,1)S(1)} copy-done((bf16[4096,512]{1,0:T(8,128)(2,1)S(1)}, bf16[4096,512]{1,0:T(8,128)(2,1)}, u32[]{:S(2)}) %copy-start.1) | copy-done | bytes 4194328
  49.7 2.2 %copy-done.2 = bf16[512,4096]{1,0:T(8,128)(2,1)S(1)} copy-done((bf16[512,4096]{1,0:T(8,128)(2,1)S(1)}, bf16[512,4096]{1,0:T(8,128)(2,1)}, u32[]{:S(2)}) %copy-start.2) | copy-done | bytes 4194328
  51.9 2.6 %mix_terms.1 = (bf16[4,64,512]{2,1,0:T(8,128)(2,1)S(1)}, bf16[4,64,512]{2,1,0:T(8,128)(2,1)S(1)}, bf16[4,64,512]{2,1,0:T(8,128)(2,1)S(1)}, bf16[4,64,512]{2,1,0:T(8,128)(2,1)S(1)}) custom-call(s32[8]{0:T(128)S(1)} %iota_xor_fusion.refs_0_.order_ref, s32[2]{0:T(128)S(1)} %pad_add_fusion.place_ref, bf16[128,512]{1,0:T(8,128)(2,1)S(1)} %queries.1.q_ref, ...), custom_call_target="tpu_custom_call" | custom-call | tf_op jit(solution)/shard_map/mix_terms/pallas_call | solution.py:249
  59.5 8.9 %collective-permute-done.18 = bf16[4,64,512]{2,1,0:T(8,128)(2,1)S(1)} collective-permute-done((bf16[4,64,512]{2,1,0:T(8,128)(2,1)S(1)}, bf16[4,64,512]{2,1,0:T(8,128)(2,1)S(1)}, u32[]{:S(2)}, u32[]{:S(2)}) %collective-permute-start.18) | collective-permute-done | bytes 262176 | tf_op jit(solution)/shard_map/ppermute | solution.py:23
  68.5 1.8 collective-permute-start.21
  70.3 2.7 %collective-permute-start.19 = (bf16[64,512]{1,0:T(8,128)(2,1)S(1)}, bf16[64,512]{1,0:T(8,128)(2,1)S(1)}, u32[]{:S(2)}, u32[]{:S(2)}) collective-permute-start(bf16[64,512]{1,0:T(8,128)(2,1)S(1)} %get-tuple-element.56), channel_id=1, source_target_pairs={{0,8},{4,12},{8,0},{12,4},{16,24},{20,28},{24,16},{28,20},{1,9},{5... | collective-permute-start | bytes 196616 | tf_op jit(solution)/shard_map/ppermute | solution.py:23
  75.3 2.2 %collective-permute-start.15 = (bf16[64,512]{1,0:T(8,128)(2,1)S(1)}, bf16[64,512]{1,0:T(8,128)(2,1)S(1)}, u32[]{:S(2)}, u32[]{:S(2)}) collective-permute-start(bf16[64,512]{1,0:T(8,128)(2,1)S(1)} %get-tuple-element.53), channel_id=1, source_target_pairs={{0,8},{4,12},{8,0},{12,4},{16,24},{20,28},{24,16},{28,20},{1,9},{5... | collective-permute-start | bytes 196616 | tf_op jit(solution)/shard_map/ppermute | solution.py:23
  79.6 2.5 %collective-permute-done.16 = bf16[64,512]{1,0:T(8,128)(2,1)S(1)} collective-permute-done((bf16[64,512]{1,0:T(8,128)(2,1)S(1)}, bf16[64,512]{1,0:T(8,128)(2,1)S(1)}, u32[]{:S(2)}, u32[]{:S(2)}) %collective-permute-start.16) | collective-permute-done | bytes 65568 | tf_op jit(solution)/shard_map/ppermute | solution.py:23
  84.1 4.6 %all-to-all-start = ((bf16[8,32,512]{2,1,0:T(8,128)(2,1)}), bf16[8,32,512]{2,1,0:T(8,128)(2,1)S(1)}, u32[]{:S(2)}, u32[]{:S(2)}) async-start(bf16[8,32,512]{2,1,0:T(8,128)(2,1)} %bitcast.22), calls=%async_computation | async-start | bytes 524288 | tf_op jit(solution)/shard_map/all_to_all | solution.py:501
  88.9 8.3 %all-to-all-done.x_ref = bf16[8,32,512]{2,1,0:T(8,128)(2,1)S(1)} async-done(((bf16[8,32,512]{2,1,0:T(8,128)(2,1)}), bf16[8,32,512]{2,1,0:T(8,128)(2,1)S(1)}, u32[]{:S(2)}, u32[]{:S(2)}) %all-to-all-start) | async-done | bytes 262176 | tf_op jit(solution)/shard_map/all_to_all | solution.py:501
  98.9 3.6 %all-to-all-start.1 = ((bf16[8,32,512]{2,1,0:T(8,128)(2,1)}), bf16[8,32,512]{2,1,0:T(8,128)(2,1)S(1)}, u32[]{:S(2)}, u32[]{:S(2)}) async-start(bf16[8,32,512]{2,1,0:T(8,128)(2,1)} %bitcast.25), calls=%async_computation.1 | async-start | bytes 524288 | tf_op jit(solution)/shard_map/all_to_all | solution.py:501
  105.5 16.7 %experts.2 = (bf16[64,4096]{1,0:T(8,128)(2,1)S(1)}, bf16[64,4096]{1,0:T(8,128)(2,1)S(1)}) custom-call(bf16[32,4096]{1,0:T(8,128)(2,1)S(1)} %normed_rows.2.refs_0_, bf16[32,4096]{1,0:T(8,128)(2,1)S(1)} %collective-permute-done.22.refs_1_, bf16[32,4096]{1,0:T(8,128)(2,1)S(1)} %collective-permute-done.23.refs_2_, ...), custom_call_target="tpu_custom_call" | custom-call | flops 5033164800 | bytes 39321600 | tf_op jit(solution)/shard_map/experts/pallas_call | solution.py:349
  124.1 7.5 %collective-permute-done.27.refs_1_ = bf16[32,4096]{1,0:T(8,128)(2,1)S(1)} collective-permute-done((bf16[32,4096]{1,0:T(8,128)(2,1)S(1)}, bf16[32,4096]{1,0:T(8,128)(2,1)S(1)}, u32[]{:S(2)}, u32[]{:S(2)}) %collective-permute-start.27) | collective-permute-done | bytes 262176 | tf_op jit(solution)/shard_map/ppermute | solution.py:23
  133.1 16.7 %experts.3 = (bf16[64,4096]{1,0:T(8,128)(2,1)S(1)}, bf16[64,4096]{1,0:T(8,128)(2,1)S(1)}) custom-call(bf16[32,4096]{1,0:T(8,128)(2,1)S(1)} %normed_rows.3.refs_0_, bf16[32,4096]{1,0:T(8,128)(2,1)S(1)} %collective-permute-done.27.refs_1_, bf16[32,4096]{1,0:T(8,128)(2,1)S(1)} %collective-permute-done.28.refs_2_, ...), custom_call_target="tpu_custom_call" | custom-call | flops 5033164800 | bytes 39321600 | tf_op jit(solution)/shard_map/experts/pallas_call | solution.py:349
  152.8 6.9 %collective-permute-done.26 = bf16[32,4096]{1,0:T(8,128)(2,1)S(1)} collective-permute-done((bf16[32,4096]{1,0:T(8,128)(2,1)}, bf16[32,4096]{1,0:T(8,128)(2,1)S(1)}, u32[]{:S(2)}, u32[]{:S(2)}) %collective-permute-start.26) | collective-permute-done | bytes 262176 | tf_op jit(solution)/shard_map/ppermute | solution.py:23
  159.8 5.0 %collective-permute-done.31 = bf16[32,4096]{1,0:T(8,128)(2,1)S(1)} collective-permute-done((bf16[32,4096]{1,0:T(8,128)(2,1)S(1)}, bf16[32,4096]{1,0:T(8,128)(2,1)S(1)}, u32[]{:S(2)}, u32[]{:S(2)}) %collective-permute-start.31) | collective-permute-done | bytes 262176 | tf_op jit(solution)/shard_map/ppermute | solution.py:23
  164.9 18.8 %all_to_all.15 = bf16[8,64,512]{2,1,0:T(8,128)(2,1)S(1)} all-to-all(bf16[8,64,512]{2,1,0:T(8,128)(2,1)S(1)} %cut_rows.1), channel_id=1, replica_groups=mesh['wide'=8,'narrow'=4] {'wide'}, dimensions={0} | all-to-all | bytes 1048576 | tf_op jit(solution)/shard_map/all_to_all | solution.py:501
  (132 shorter events, 48.2 us)
Async XLA Ops:
  0.0 10.7 %collective-permute-start.3 = (bf16[128,512]{1,0:T(8,128)(2,1)}, bf16[128,512]{1,0:T(8,128)(2,1)S(1)}, u32[]{:S(2)}, u32[]{:S(2)}) collective-permute-start(bf16[128,512]{1,0:T(8,128)(2,1)} %refs_3_.1), channel_id=1, source_target_pairs={{0,16},{4,20},{8,24},{12,28},{16,0},{20,4},{24,8},{28,12},{1,17},{... | collective-permute-start | bytes 393224 | tf_op jit(solution)/shard_map/ppermute | solution.py:23
  4.1 17.7 %collective-permute-start = (bf16[128,512]{1,0:T(8,128)(2,1)}, bf16[128,512]{1,0:T(8,128)(2,1)S(1)}, u32[]{:S(2)}, u32[]{:S(2)}) collective-permute-start(bf16[128,512]{1,0:T(8,128)(2,1)} %refs_3_.1), channel_id=1, source_target_pairs={{0,4},{4,0},{8,12},{12,8},{16,20},{20,16},{24,28},{28,24},{1,5},{5... | collective-permute-start | bytes 393224 | tf_op jit(solution)/shard_map/ppermute | solution.py:23
  5.6 7.5 %collective-permute-start.1 = (bf16[128,512]{1,0:T(8,128)(2,1)}, bf16[128,512]{1,0:T(8,128)(2,1)S(1)}, u32[]{:S(2)}, u32[]{:S(2)}) collective-permute-start(bf16[128,512]{1,0:T(8,128)(2,1)} %refs_3_.1), channel_id=1, source_target_pairs={{0,8},{4,12},{8,0},{12,4},{16,24},{20,28},{24,16},{28,20},{1,9},{5... | collective-permute-start | bytes 393224 | tf_op jit(solution)/shard_map/ppermute | solution.py:23
  11.5 10.2 %collective-permute-start.4 = (bf16[128,512]{1,0:T(8,128)(2,1)S(1)}, bf16[128,512]{1,0:T(8,128)(2,1)S(1)}, u32[]{:S(2)}, u32[]{:S(2)}) collective-permute-start(bf16[128,512]{1,0:T(8,128)(2,1)S(1)} %collective-permute-done.3.refs_10_.refs_9_), channel_id=1, source_target_pairs={{0,4},{4,0},{8,12},{12,8},{16,20},{20,16},{24,28},{28,24},{1,5},{5... | collective-permute-start | bytes 393224 | tf_op jit(solution)/shard_map/ppermute | solution.py:23
  13.1 8.7 %collective-permute-start.2 = (bf16[128,512]{1,0:T(8,128)(2,1)S(1)}, bf16[128,512]{1,0:T(8,128)(2,1)S(1)}, u32[]{:S(2)}, u32[]{:S(2)}) collective-permute-start(bf16[128,512]{1,0:T(8,128)(2,1)S(1)} %collective-permute-done.1.refs_8_.refs_7_), channel_id=1, source_target_pairs={{0,4},{4,0},{8,12},{12,8},{16,20},{20,16},{24,28},{28,24},{1,5},{5... | collective-permute-start | bytes 393224 | tf_op jit(solution)/shard_map/ppermute | solution.py:23
  15.7 6.7 %collective-permute-start.6 = (bf16[128,512]{1,0:T(8,128)(2,1)S(1)}, bf16[128,512]{1,0:T(8,128)(2,1)S(1)}, u32[]{:S(2)}, u32[]{:S(2)}) collective-permute-start(bf16[128,512]{1,0:T(8,128)(2,1)S(1)} %collective-permute-done.5.refs_12_.refs_11_), channel_id=1, source_target_pairs={{0,4},{4,0},{8,12},{12,8},{16,20},{20,16},{24,28},{28,24},{1,5},{5... | collective-permute-start | bytes 393224 | tf_op jit(solution)/shard_map/ppermute | solution.py:23
  24.0 7.2 %collective-permute-start.7 = (bf16[4,2,128,128]{3,2,1,0:T(8,128)(2,1)S(1)}, bf16[4,2,128,128]{3,2,1,0:T(8,128)(2,1)S(1)}, u32[]{:S(2)}, u32[]{:S(2)}) collective-permute-start(bf16[4,2,128,128]{3,2,1,0:T(8,128)(2,1)S(1)} %get-tuple-element.36), channel_id=1, source_target_pairs={{0,4},{4,0},{8,12},{12,8},{16,20},{20,16},{24,28},{28,24},{1,5},{5... | collective-permute-start | bytes 786440 | tf_op jit(solution)/shard_map/ppermute | solution.py:23
  31.2 6.5 %collective-permute-start.10 = (bf16[2,128,128]{2,1,0:T(8,128)(2,1)S(1)}, bf16[2,128,128]{2,1,0:T(8,128)(2,1)S(1)}, u32[]{:S(2)}, u32[]{:S(2)}) collective-permute-start(bf16[2,128,128]{2,1,0:T(8,128)(2,1)S(1)} %get-tuple-element.60), channel_id=1, source_target_pairs={{0,24},{4,28},{8,16},{12,20},{16,8},{20,12},{24,0},{28,4},{1,25},{... | collective-permute-start | bytes 196616 | tf_op jit(solution)/shard_map/ppermute | solution.py:23
  54.5 18.5 %collective-permute-start.14 = (bf16[4,64,512]{2,1,0:T(8,128)(2,1)S(1)}, bf16[4,64,512]{2,1,0:T(8,128)(2,1)S(1)}, u32[]{:S(2)}, u32[]{:S(2)}) collective-permute-start(bf16[4,64,512]{2,1,0:T(8,128)(2,1)S(1)} %get-tuple-element.38), channel_id=1, source_target_pairs={{0,4},{4,0},{8,12},{12,8},{16,20},{20,16},{24,28},{28,24},{1,5},{5... | collective-permute-start | bytes 786440 | tf_op jit(solution)/shard_map/ppermute | solution.py:23
  58.7 9.8 %collective-permute-start.18 = (bf16[4,64,512]{2,1,0:T(8,128)(2,1)S(1)}, bf16[4,64,512]{2,1,0:T(8,128)(2,1)S(1)}, u32[]{:S(2)}, u32[]{:S(2)}) collective-permute-start(bf16[4,64,512]{2,1,0:T(8,128)(2,1)S(1)} %get-tuple-element.40), channel_id=1, source_target_pairs={{0,4},{4,0},{8,12},{12,8},{16,20},{20,16},{24,28},{28,24},{1,5},{5... | collective-permute-start | bytes 786440 | tf_op jit(solution)/shard_map/ppermute | solution.py:23
  68.5 6.8 %collective-permute-start.21 = (bf16[64,512]{1,0:T(8,128)(2,1)S(1)}, bf16[64,512]{1,0:T(8,128)(2,1)S(1)}, u32[]{:S(2)}, u32[]{:S(2)}) collective-permute-start(bf16[64,512]{1,0:T(8,128)(2,1)S(1)} %get-tuple-element.57), channel_id=1, source_target_pairs={{0,24},{4,28},{8,16},{12,20},{16,8},{20,12},{24,0},{28,4},{1,25},{... | collective-permute-start | bytes 196616 | tf_op jit(solution)/shard_map/ppermute | solution.py:23
  70.3 8.4 %collective-permute-start.20 = (bf16[64,512]{1,0:T(8,128)(2,1)S(1)}, bf16[64,512]{1,0:T(8,128)(2,1)S(1)}, u32[]{:S(2)}, u32[]{:S(2)}) collective-permute-start(bf16[64,512]{1,0:T(8,128)(2,1)S(1)} %get-tuple-element.58), channel_id=1, source_target_pairs={{0,16},{4,20},{8,24},{12,28},{16,0},{20,4},{24,8},{28,12},{1,17},{... | collective-permute-start | bytes 196616 | tf_op jit(solution)/shard_map/ppermute | solution.py:23
  70.3 8.4 %collective-permute-start.19 = (bf16[64,512]{1,0:T(8,128)(2,1)S(1)}, bf16[64,512]{1,0:T(8,128)(2,1)S(1)}, u32[]{:S(2)}, u32[]{:S(2)}) collective-permute-start(bf16[64,512]{1,0:T(8,128)(2,1)S(1)} %get-tuple-element.56), channel_id=1, source_target_pairs={{0,8},{4,12},{8,0},{12,4},{16,24},{20,28},{24,16},{28,20},{1,9},{5... | collective-permute-start | bytes 196616 | tf_op jit(solution)/shard_map/ppermute | solution.py:23
  73.0 6.5 %collective-permute-start.17 = (bf16[64,512]{1,0:T(8,128)(2,1)S(1)}, bf16[64,512]{1,0:T(8,128)(2,1)S(1)}, u32[]{:S(2)}, u32[]{:S(2)}) collective-permute-start(bf16[64,512]{1,0:T(8,128)(2,1)S(1)} %get-tuple-element.54), channel_id=1, source_target_pairs={{0,24},{4,28},{8,16},{12,20},{16,8},{20,12},{24,0},{28,4},{1,25},{... | collective-permute-start | bytes 196616 | tf_op jit(solution)/shard_map/ppermute | solution.py:23
  74.8 7.2 %collective-permute-start.16 = (bf16[64,512]{1,0:T(8,128)(2,1)S(1)}, bf16[64,512]{1,0:T(8,128)(2,1)S(1)}, u32[]{:S(2)}, u32[]{:S(2)}) collective-permute-start(bf16[64,512]{1,0:T(8,128)(2,1)S(1)} %get-tuple-element.55), channel_id=1, source_target_pairs={{0,16},{4,20},{8,24},{12,28},{16,0},{20,4},{24,8},{28,12},{1,17},{... | collective-permute-start | bytes 196616 | tf_op jit(solution)/shard_map/ppermute | solution.py:23
  75.3 6.7 %collective-permute-start.15 = (bf16[64,512]{1,0:T(8,128)(2,1)S(1)}, bf16[64,512]{1,0:T(8,128)(2,1)S(1)}, u32[]{:S(2)}, u32[]{:S(2)}) collective-permute-start(bf16[64,512]{1,0:T(8,128)(2,1)S(1)} %get-tuple-element.53), channel_id=1, source_target_pairs={{0,8},{4,12},{8,0},{12,4},{16,24},{20,28},{24,16},{28,20},{1,9},{5... | collective-permute-start | bytes 196616 | tf_op jit(solution)/shard_map/ppermute | solution.py:23
  84.1 13.2 %all-to-all-start = ((bf16[8,32,512]{2,1,0:T(8,128)(2,1)}), bf16[8,32,512]{2,1,0:T(8,128)(2,1)S(1)}, u32[]{:S(2)}, u32[]{:S(2)}) async-start(bf16[8,32,512]{2,1,0:T(8,128)(2,1)} %bitcast.22), calls=%async_computation | async-start | bytes 524288 | tf_op jit(solution)/shard_map/all_to_all | solution.py:501
  97.6 6.4 %collective-permute-start.22 = (bf16[32,4096]{1,0:T(8,128)(2,1)S(1)}, bf16[32,4096]{1,0:T(8,128)(2,1)S(1)}, u32[]{:S(2)}, u32[]{:S(2)}) collective-permute-start(bf16[32,4096]{1,0:T(8,128)(2,1)S(1)} %normed_rows.2.refs_0_), channel_id=1, source_target_pairs={{0,2},{1,3},{2,0},{3,1},{4,6},{5,7},{6,4},{7,5},{8,10},{9,11},{10,... | collective-permute-start | bytes 786440 | tf_op jit(solution)/shard_map/ppermute | solution.py:23
  98.9 23.7 %all-to-all-start.1 = ((bf16[8,32,512]{2,1,0:T(8,128)(2,1)}), bf16[8,32,512]{2,1,0:T(8,128)(2,1)S(1)}, u32[]{:S(2)}, u32[]{:S(2)}) async-start(bf16[8,32,512]{2,1,0:T(8,128)(2,1)} %bitcast.25), calls=%async_computation.1 | async-start | bytes 524288 | tf_op jit(solution)/shard_map/all_to_all | solution.py:501
  122.2 9.3 %collective-permute-start.25 = (bf16[64,4096]{1,0:T(8,128)(2,1)S(1)}, bf16[64,4096]{1,0:T(8,128)(2,1)S(1)}, u32[]{:S(2)}, u32[]{:S(2)}) collective-permute-start(bf16[64,4096]{1,0:T(8,128)(2,1)S(1)} %get-tuple-element.44), channel_id=1, source_target_pairs={{0,1},{1,0},{2,3},{3,2},{4,5},{5,4},{6,7},{7,6},{8,9},{9,8},{10,11... | collective-permute-start | bytes 1572872 | tf_op jit(solution)/shard_map/ppermute | solution.py:23
  122.9 8.7 %collective-permute-start.27 = (bf16[32,4096]{1,0:T(8,128)(2,1)S(1)}, bf16[32,4096]{1,0:T(8,128)(2,1)S(1)}, u32[]{:S(2)}, u32[]{:S(2)}) collective-permute-start(bf16[32,4096]{1,0:T(8,128)(2,1)S(1)} %normed_rows.3.refs_0_), channel_id=1, source_target_pairs={{0,2},{1,3},{2,0},{3,1},{4,6},{5,7},{6,4},{7,5},{8,10},{9,11},{10,... | collective-permute-start | bytes 786440 | tf_op jit(solution)/shard_map/ppermute | solution.py:23
  123.8 8.6 %collective-permute-start.28 = (bf16[32,4096]{1,0:T(8,128)(2,1)S(1)}, bf16[32,4096]{1,0:T(8,128)(2,1)S(1)}, u32[]{:S(2)}, u32[]{:S(2)}) collective-permute-start(bf16[32,4096]{1,0:T(8,128)(2,1)S(1)} %normed_rows.3.refs_0_), channel_id=1, source_target_pairs={{0,1},{1,0},{2,3},{3,2},{4,5},{5,4},{6,7},{7,6},{8,9},{9,8},{10,11... | collective-permute-start | bytes 786440 | tf_op jit(solution)/shard_map/ppermute | solution.py:23
  150.3 9.5 %collective-permute-start.26 = (bf16[32,4096]{1,0:T(8,128)(2,1)}, bf16[32,4096]{1,0:T(8,128)(2,1)S(1)}, u32[]{:S(2)}, u32[]{:S(2)}) collective-permute-start(bf16[32,4096]{1,0:T(8,128)(2,1)} %slice.237), channel_id=1, source_target_pairs={{0,2},{1,3},{2,0},{3,1},{4,6},{5,7},{6,4},{7,5},{8,10},{9,11},{10,... | collective-permute-start | bytes 786440 | tf_op jit(solution)/shard_map/ppermute | solution.py:23
  151.9 12.9 %collective-permute-start.31 = (bf16[32,4096]{1,0:T(8,128)(2,1)S(1)}, bf16[32,4096]{1,0:T(8,128)(2,1)S(1)}, u32[]{:S(2)}, u32[]{:S(2)}) collective-permute-start(bf16[32,4096]{1,0:T(8,128)(2,1)S(1)} %slice.236), channel_id=1, source_target_pairs={{0,2},{1,3},{2,0},{3,1},{4,6},{5,7},{6,4},{7,5},{8,10},{9,11},{10,... | collective-permute-start | bytes 786440 | tf_op jit(solution)/shard_map/ppermute | solution.py:23
  (21 other events, 207.9 us)

commit v2 on v1

--- a/solution.py
+++ b/solution.py
@@ -477,9 +477,9 @@
     routing = expert_ids.reshape(blocks, TOK_BLOCK, 2)
     target = slot_targets(routing, experts, CAPD).reshape(row_count, 2)
     token_block = jnp.arange(row_count, dtype=jnp.int32) // TOK_BLOCK
-    dest_expert = (jnp.arange(wide_count, dtype=jnp.int32) * slots_here // SPLIT)[:, None] + jnp.arange(
+    dest_expert = jnp.arange(wide_count, dtype=jnp.int32) * slots_here // SPLIT + jnp.arange(
         experts_here, dtype=jnp.int32
-    )
+    )[:, None]
     expert_rows = blocks * CAPD
     in_expert = jnp.arange(expert_rows, dtype=jnp.int32)
     row_slot = dest_expert[:, :, None, None] * CAPD + (in_expert % CAPD)[:, None]
@@ -491,7 +491,7 @@
     residual = (hidden.astype(f32) + jnp.concatenate(mixed)).astype(bf16)
 
     mine = lambda values: lax.dynamic_index_in_dim(
-        values.astype(f32), wide_index, 0, keepdims=False
+        values.astype(f32), wide_index, 1, keepdims=False
     )
     my_first, my_second = mine(first_pick), mine(second_pick)
     ids_onehot = (expert_ids[:, :, None] == jnp.arange(experts, dtype=jnp.int32)).astype(f32)
@@ -516,10 +516,12 @@
         return own
 
     gate_rows, up_rows = jnp.swapaxes(gate_weight, 1, 2), jnp.swapaxes(up_weight, 1, 2)
-    chosen = jnp.dot(
-        picks.transpose(1, 0, 2, 3).reshape(-1, row_count), residual, preferred_element_type=f32
-    ).astype(bf16)
-    chosen = chosen.reshape(experts_here, wide_count, expert_rows, feature_share)
+    chosen = [
+        jnp.dot(picks[e].reshape(-1, row_count), residual, preferred_element_type=f32)
+        .astype(bf16)
+        .reshape(wide_count, expert_rows, feature_share)
+        for e in range(experts_here)
+    ]
     arrived = []
     for e in range(experts_here):
         arrived.append(exchange(after(chosen[e], *arrived[-1:])))
@@ -539,7 +541,7 @@
     own_rows = [finish(*sums[e], narrow_count // 2) for e in range(experts_here)]
     back = exchange(cut_rows(own_rows, [w[:, None] for w in row_weights], wide_count))
     mixture = lax.dot_general(
-        picks.reshape(-1, row_count),
+        picks.transpose(1, 0, 2, 3).reshape(-1, row_count),
         back.reshape(-1, feature_share),
         (((0,), (0,)), ((), ())),
         preferred_element_type=f32,

time: 185 us -> 179 us (0.968)
  waiting for transfers between devices: 62 us -> 57 us
    ppermute x32, waiting for transfers between devices: 53.7 us -> 49.1 us  [swap(): return lax.ppermute(values, axis, [(i, i ^ distance) for i in range(count)])]
    unnamed x22 -> x20, local copies, waits for them, and re-layouts: 11.6 us -> 11.6 us
  transfers between devices with their start and end apart: 34 -> 34, of which waited for: 19 -> 19; matrix products, arithmetic and copies ran while one was open for 3% -> 3% of each run, Pallas kernels for 10% -> 11%
where the time goes in v2:
time: 179 us; the launch traced here: 178 us
  waiting for transfers between devices  57 us (32%)
  starting transfers between devices  41.4 us (23%)
  Pallas kernels  40.3 us (23%)
  blocking collectives  18.6 us (10%)
  local copies, waits for them, and re-layouts  13.2 us (7%)
  other arithmetic  4 us (2%)
  matrix products  3.46 us (2%)
    ppermute x32, waiting for transfers between devices, swap(): return lax.ppermute(values, axis, [(i, i ^ distance) for i in range(count)])  49.1 us
    ppermute x32, starting transfers between devices, swap(): return lax.ppermute(values, axis, [(i, i ^ distance) for i in range(count)])  33.9 us
    pallas_call x2, Pallas kernels, expert_partial(): pl.pallas_call(kernel, grid=(parts, steps), in_specs=[pl.BlockSpec(piece....  33.4 us
    all_to_all x1, blocking collectives, exchange(): lax.all_to_all(blocks_of, 'wide', split_axis=0, concat_axis=0, tiled=True)  18.6 us
    unnamed x20, local copies, waits for them, and re-layouts  11.6 us
    all_to_all x2, waiting for transfers between devices, exchange(): lax.all_to_all(blocks_of, 'wide', split_axis=0, concat_axis=0, tiled=True)  7.93 us
    all_to_all x2, starting transfers between devices, exchange(): lax.all_to_all(blocks_of, 'wide', split_axis=0, concat_axis=0, tiled=True)  7.5 us
  transfers between devices with their start and end apart: 34, of which 19 were waited for; matrix products, arithmetic and copies ran while one was open for 3% of the time, Pallas kernels for 11%

profile of v2, /device:TPU:0, one launch (start us, length us, event | category | flops | bytes accessed | tf_op | source)
XLA Modules:
  0.0 178.4 jit_solution(14880322586706566286)
XLA Ops:
  0.0 4.1 %collective-permute-start.3 = (bf16[128,512]{1,0:T(8,128)(2,1)}, bf16[128,512]{1,0:T(8,128)(2,1)S(1)}, u32[]{:S(2)}, u32[]{:S(2)}) collective-permute-start(bf16[128,512]{1,0:T(8,128)(2,1)} %refs_3_.1), channel_id=1, source_target_pairs={{0,16},{4,20},{8,24},{12,28},{16,0},{20,4},{24,8},{28,12},{1,17},{... | collective-permute-start | bytes 393224 | tf_op jit(solution)/shard_map/ppermute | solution.py:23
  7.1 3.5 %collective-permute-done.3.refs_10_.refs_9_ = bf16[128,512]{1,0:T(8,128)(2,1)S(1)} collective-permute-done((bf16[128,512]{1,0:T(8,128)(2,1)}, bf16[128,512]{1,0:T(8,128)(2,1)S(1)}, u32[]{:S(2)}, u32[]{:S(2)}) %collective-permute-start.3) | collective-permute-done | bytes 131104 | tf_op jit(solution)/shard_map/ppermute | solution.py:23
  13.6 2.1 %collective-permute-done.5.refs_12_.refs_11_ = bf16[128,512]{1,0:T(8,128)(2,1)S(1)} collective-permute-done((bf16[128,512]{1,0:T(8,128)(2,1)S(1)}, bf16[128,512]{1,0:T(8,128)(2,1)S(1)}, u32[]{:S(2)}, u32[]{:S(2)}) %collective-permute-start.5) | collective-permute-done | bytes 131104 | tf_op jit(solution)/shard_map/ppermute | solution.py:23
  22.3 1.6 kv_terms.1
  25.5 5.5 %collective-permute-done.7 = bf16[4,2,128,128]{3,2,1,0:T(8,128)(2,1)S(1)} collective-permute-done((bf16[4,2,128,128]{3,2,1,0:T(8,128)(2,1)S(1)}, bf16[4,2,128,128]{3,2,1,0:T(8,128)(2,1)S(1)}, u32[]{:S(2)}, u32[]{:S(2)}) %collective-permute-start.7) | collective-permute-done | bytes 262176 | tf_op jit(solution)/shard_map/ppermute | solution.py:23
  31.1 3.3 %collective-permute-start.10 = (bf16[2,128,128]{2,1,0:T(8,128)(2,1)S(1)}, bf16[2,128,128]{2,1,0:T(8,128)(2,1)S(1)}, u32[]{:S(2)}, u32[]{:S(2)}) collective-permute-start(bf16[2,128,128]{2,1,0:T(8,128)(2,1)S(1)} %get-tuple-element.58), channel_id=1, source_target_pairs={{0,24},{4,28},{8,16},{12,20},{16,8},{20,12},{24,0},{28,4},{1,25},{... | collective-permute-start | bytes 196616 | tf_op jit(solution)/shard_map/ppermute | solution.py:23
  35.6 2.1 %collective-permute-done.10 = bf16[2,128,128]{2,1,0:T(8,128)(2,1)S(1)} collective-permute-done((bf16[2,128,128]{2,1,0:T(8,128)(2,1)S(1)}, bf16[2,128,128]{2,1,0:T(8,128)(2,1)S(1)}, u32[]{:S(2)}, u32[]{:S(2)}) %collective-permute-start.10) | collective-permute-done | bytes 65568 | tf_op jit(solution)/shard_map/ppermute | solution.py:23
  40.3 1.6 collective-permute-start.11
  45.9 2.2 %copy-done.1 = bf16[4096,512]{1,0:T(8,128)(2,1)S(1)} copy-done((bf16[4096,512]{1,0:T(8,128)(2,1)S(1)}, bf16[4096,512]{1,0:T(8,128)(2,1)}, u32[]{:S(2)}) %copy-start.1) | copy-done | bytes 4194328
  49.6 2.2 %copy-done.2 = bf16[512,4096]{1,0:T(8,128)(2,1)S(1)} copy-done((bf16[512,4096]{1,0:T(8,128)(2,1)S(1)}, bf16[512,4096]{1,0:T(8,128)(2,1)}, u32[]{:S(2)}) %copy-start.2) | copy-done | bytes 4194328
  51.8 2.6 %mix_terms.1 = (bf16[4,64,512]{2,1,0:T(8,128)(2,1)S(1)}, bf16[4,64,512]{2,1,0:T(8,128)(2,1)S(1)}, bf16[4,64,512]{2,1,0:T(8,128)(2,1)S(1)}, bf16[4,64,512]{2,1,0:T(8,128)(2,1)S(1)}) custom-call(s32[8]{0:T(128)S(1)} %iota_xor_fusion.refs_0_.order_ref, s32[2]{0:T(128)S(1)} %pad_add_fusion.place_ref, bf16[128,512]{1,0:T(8,128)(2,1)S(1)} %queries.1.q_ref, ...), custom_call_target="tpu_custom_call" | custom-call | tf_op jit(solution)/shard_map/mix_terms/pallas_call | solution.py:249
  59.4 4.2 %collective-permute-done.14 = bf16[4,64,512]{2,1,0:T(8,128)(2,1)S(1)} collective-permute-done((bf16[4,64,512]{2,1,0:T(8,128)(2,1)S(1)}, bf16[4,64,512]{2,1,0:T(8,128)(2,1)S(1)}, u32[]{:S(2)}, u32[]{:S(2)}) %collective-permute-start.14) | collective-permute-done | bytes 262176 | tf_op jit(solution)/shard_map/ppermute | solution.py:23
  65.6 2.5 %collective-permute-start.17 = (bf16[64,512]{1,0:T(8,128)(2,1)S(1)}, bf16[64,512]{1,0:T(8,128)(2,1)S(1)}, u32[]{:S(2)}, u32[]{:S(2)}) collective-permute-start(bf16[64,512]{1,0:T(8,128)(2,1)S(1)} %get-tuple-element.52), channel_id=1, source_target_pairs={{0,24},{4,28},{8,16},{12,20},{16,8},{20,12},{24,0},{28,4},{1,25},{... | collective-permute-start | bytes 196616 | tf_op jit(solution)/shard_map/ppermute | solution.py:23
  70.6 2.2 %collective-permute-start.21 = (bf16[64,512]{1,0:T(8,128)(2,1)S(1)}, bf16[64,512]{1,0:T(8,128)(2,1)S(1)}, u32[]{:S(2)}, u32[]{:S(2)}) collective-permute-start(bf16[64,512]{1,0:T(8,128)(2,1)S(1)} %get-tuple-element.55), channel_id=1, source_target_pairs={{0,24},{4,28},{8,16},{12,20},{16,8},{20,12},{24,0},{28,4},{1,25},{... | collective-permute-start | bytes 196616 | tf_op jit(solution)/shard_map/ppermute | solution.py:23
  73.5 3.8 %collective-permute-done.20 = bf16[64,512]{1,0:T(8,128)(2,1)S(1)} collective-permute-done((bf16[64,512]{1,0:T(8,128)(2,1)S(1)}, bf16[64,512]{1,0:T(8,128)(2,1)S(1)}, u32[]{:S(2)}, u32[]{:S(2)}) %collective-permute-start.20) | collective-permute-done | bytes 65568 | tf_op jit(solution)/shard_map/ppermute | solution.py:23
  79.2 3.9 %all-to-all-start = ((bf16[8,32,512]{2,1,0:T(8,128)(2,1)}), bf16[8,32,512]{2,1,0:T(8,128)(2,1)S(1)}, u32[]{:S(2)}, u32[]{:S(2)}) async-start(bf16[8,32,512]{2,1,0:T(8,128)(2,1)} %bitcast.22), calls=%async_computation | async-start | bytes 524288 | tf_op jit(solution)/shard_map/all_to_all | solution.py:501
  83.4 7.9 %all-to-all-done.x_ref = bf16[8,32,512]{2,1,0:T(8,128)(2,1)S(1)} async-done(((bf16[8,32,512]{2,1,0:T(8,128)(2,1)}), bf16[8,32,512]{2,1,0:T(8,128)(2,1)S(1)}, u32[]{:S(2)}, u32[]{:S(2)}) %all-to-all-start) | async-done | bytes 262176 | tf_op jit(solution)/shard_map/all_to_all | solution.py:501
  93.5 3.6 %all-to-all-start.1 = ((bf16[8,32,512]{2,1,0:T(8,128)(2,1)}), bf16[8,32,512]{2,1,0:T(8,128)(2,1)S(1)}, u32[]{:S(2)}, u32[]{:S(2)}) async-start(bf16[8,32,512]{2,1,0:T(8,128)(2,1)} %bitcast.26), calls=%async_computation.1 | async-start | bytes 524288 | tf_op jit(solution)/shard_map/all_to_all | solution.py:501
  99.7 16.7 %experts.2 = (bf16[64,4096]{1,0:T(8,128)(2,1)S(1)}, bf16[64,4096]{1,0:T(8,128)(2,1)S(1)}) custom-call(bf16[32,4096]{1,0:T(8,128)(2,1)S(1)} %normed_rows.2.refs_0_, bf16[32,4096]{1,0:T(8,128)(2,1)S(1)} %collective-permute-done.22.refs_1_, bf16[32,4096]{1,0:T(8,128)(2,1)S(1)} %collective-permute-done.23.refs_2_, ...), custom_call_target="tpu_custom_call" | custom-call | flops 5033164800 | bytes 39321600 | tf_op jit(solution)/shard_map/experts/pallas_call | solution.py:349
  118.1 7.6 %collective-permute-done.27.refs_1_ = bf16[32,4096]{1,0:T(8,128)(2,1)S(1)} collective-permute-done((bf16[32,4096]{1,0:T(8,128)(2,1)S(1)}, bf16[32,4096]{1,0:T(8,128)(2,1)S(1)}, u32[]{:S(2)}, u32[]{:S(2)}) %collective-permute-start.27) | collective-permute-done | bytes 262176 | tf_op jit(solution)/shard_map/ppermute | solution.py:23
  127.2 16.7 %experts.3 = (bf16[64,4096]{1,0:T(8,128)(2,1)S(1)}, bf16[64,4096]{1,0:T(8,128)(2,1)S(1)}) custom-call(bf16[32,4096]{1,0:T(8,128)(2,1)S(1)} %normed_rows.3.refs_0_, bf16[32,4096]{1,0:T(8,128)(2,1)S(1)} %collective-permute-done.27.refs_1_, bf16[32,4096]{1,0:T(8,128)(2,1)S(1)} %collective-permute-done.28.refs_2_, ...), custom_call_target="tpu_custom_call" | custom-call | flops 5033164800 | bytes 39321600 | tf_op jit(solution)/shard_map/experts/pallas_call | solution.py:349
  146.7 6.9 %collective-permute-done.26 = bf16[32,4096]{1,0:T(8,128)(2,1)S(1)} collective-permute-done((bf16[32,4096]{1,0:T(8,128)(2,1)S(1)}, bf16[32,4096]{1,0:T(8,128)(2,1)S(1)}, u32[]{:S(2)}, u32[]{:S(2)}) %collective-permute-start.26) | collective-permute-done | bytes 262176 | tf_op jit(solution)/shard_map/ppermute | solution.py:23
  153.7 5.0 %collective-permute-done.31 = bf16[32,4096]{1,0:T(8,128)(2,1)S(1)} collective-permute-done((bf16[32,4096]{1,0:T(8,128)(2,1)S(1)}, bf16[32,4096]{1,0:T(8,128)(2,1)S(1)}, u32[]{:S(2)}, u32[]{:S(2)}) %collective-permute-start.31) | collective-permute-done | bytes 262176 | tf_op jit(solution)/shard_map/ppermute | solution.py:23
  158.9 18.6 %all_to_all.15 = bf16[8,64,512]{2,1,0:T(8,128)(2,1)S(1)} all-to-all(bf16[8,64,512]{2,1,0:T(8,128)(2,1)S(1)} %cut_rows.1), channel_id=1, replica_groups=mesh['wide'=8,'narrow'=4] {'wide'}, dimensions={0} | all-to-all | bytes 1048576 | tf_op jit(solution)/shard_map/all_to_all | solution.py:501
  (131 shorter events, 47.7 us)
Async XLA Ops:
  0.0 10.7 %collective-permute-start.3 = (bf16[128,512]{1,0:T(8,128)(2,1)}, bf16[128,512]{1,0:T(8,128)(2,1)S(1)}, u32[]{:S(2)}, u32[]{:S(2)}) collective-permute-start(bf16[128,512]{1,0:T(8,128)(2,1)} %refs_3_.1), channel_id=1, source_target_pairs={{0,16},{4,20},{8,24},{12,28},{16,0},{20,4},{24,8},{28,12},{1,17},{... | collective-permute-start | bytes 393224 | tf_op jit(solution)/shard_map/ppermute | solution.py:23
  4.1 9.0 %collective-permute-start.1 = (bf16[128,512]{1,0:T(8,128)(2,1)}, bf16[128,512]{1,0:T(8,128)(2,1)S(1)}, u32[]{:S(2)}, u32[]{:S(2)}) collective-permute-start(bf16[128,512]{1,0:T(8,128)(2,1)} %refs_3_.1), channel_id=1, source_target_pairs={{0,8},{4,12},{8,0},{12,4},{16,24},{20,28},{24,16},{28,20},{1,9},{5... | collective-permute-start | bytes 393224 | tf_op jit(solution)/shard_map/ppermute | solution.py:23
  5.6 16.1 %collective-permute-start = (bf16[128,512]{1,0:T(8,128)(2,1)}, bf16[128,512]{1,0:T(8,128)(2,1)S(1)}, u32[]{:S(2)}, u32[]{:S(2)}) collective-permute-start(bf16[128,512]{1,0:T(8,128)(2,1)} %refs_3_.1), channel_id=1, source_target_pairs={{0,4},{4,0},{8,12},{12,8},{16,20},{20,16},{24,28},{28,24},{1,5},{5... | collective-permute-start | bytes 393224 | tf_op jit(solution)/shard_map/ppermute | solution.py:23
  11.5 10.2 %collective-permute-start.4 = (bf16[128,512]{1,0:T(8,128)(2,1)S(1)}, bf16[128,512]{1,0:T(8,128)(2,1)S(1)}, u32[]{:S(2)}, u32[]{:S(2)}) collective-permute-start(bf16[128,512]{1,0:T(8,128)(2,1)S(1)} %collective-permute-done.3.refs_10_.refs_9_), channel_id=1, source_target_pairs={{0,4},{4,0},{8,12},{12,8},{16,20},{20,16},{24,28},{28,24},{1,5},{5... | collective-permute-start | bytes 393224 | tf_op jit(solution)/shard_map/ppermute | solution.py:23
  13.1 8.7 %collective-permute-start.2 = (bf16[128,512]{1,0:T(8,128)(2,1)S(1)}, bf16[128,512]{1,0:T(8,128)(2,1)S(1)}, u32[]{:S(2)}, u32[]{:S(2)}) collective-permute-start(bf16[128,512]{1,0:T(8,128)(2,1)S(1)} %collective-permute-done.1.refs_8_.refs_7_), channel_id=1, source_target_pairs={{0,4},{4,0},{8,12},{12,8},{16,20},{20,16},{24,28},{28,24},{1,5},{5... | collective-permute-start | bytes 393224 | tf_op jit(solution)/shard_map/ppermute | solution.py:23
  15.7 6.7 %collective-permute-start.6 = (bf16[128,512]{1,0:T(8,128)(2,1)S(1)}, bf16[128,512]{1,0:T(8,128)(2,1)S(1)}, u32[]{:S(2)}, u32[]{:S(2)}) collective-permute-start(bf16[128,512]{1,0:T(8,128)(2,1)S(1)} %collective-permute-done.5.refs_12_.refs_11_), channel_id=1, source_target_pairs={{0,4},{4,0},{8,12},{12,8},{16,20},{20,16},{24,28},{28,24},{1,5},{5... | collective-permute-start | bytes 393224 | tf_op jit(solution)/shard_map/ppermute | solution.py:23
  23.9 7.2 %collective-permute-start.7 = (bf16[4,2,128,128]{3,2,1,0:T(8,128)(2,1)S(1)}, bf16[4,2,128,128]{3,2,1,0:T(8,128)(2,1)S(1)}, u32[]{:S(2)}, u32[]{:S(2)}) collective-permute-start(bf16[4,2,128,128]{3,2,1,0:T(8,128)(2,1)S(1)} %get-tuple-element.36), channel_id=1, source_target_pairs={{0,4},{4,0},{8,12},{12,8},{16,20},{20,16},{24,28},{28,24},{1,5},{5... | collective-permute-start | bytes 786440 | tf_op jit(solution)/shard_map/ppermute | solution.py:23
  31.1 6.6 %collective-permute-start.10 = (bf16[2,128,128]{2,1,0:T(8,128)(2,1)S(1)}, bf16[2,128,128]{2,1,0:T(8,128)(2,1)S(1)}, u32[]{:S(2)}, u32[]{:S(2)}) collective-permute-start(bf16[2,128,128]{2,1,0:T(8,128)(2,1)S(1)} %get-tuple-element.58), channel_id=1, source_target_pairs={{0,24},{4,28},{8,16},{12,20},{16,8},{20,12},{24,0},{28,4},{1,25},{... | collective-permute-start | bytes 196616 | tf_op jit(solution)/shard_map/ppermute | solution.py:23
  35.0 5.2 %collective-permute-start.9 = (bf16[2,128,128]{2,1,0:T(8,128)(2,1)S(1)}, bf16[2,128,128]{2,1,0:T(8,128)(2,1)S(1)}, u32[]{:S(2)}, u32[]{:S(2)}) collective-permute-start(bf16[2,128,128]{2,1,0:T(8,128)(2,1)S(1)} %get-tuple-element.59), channel_id=1, source_target_pairs={{0,16},{4,20},{8,24},{12,28},{16,0},{20,4},{24,8},{28,12},{1,17},{... | collective-permute-start | bytes 196616 | tf_op jit(solution)/shard_map/ppermute | solution.py:23
  54.3 9.2 %collective-permute-start.14 = (bf16[4,64,512]{2,1,0:T(8,128)(2,1)S(1)}, bf16[4,64,512]{2,1,0:T(8,128)(2,1)S(1)}, u32[]{:S(2)}, u32[]{:S(2)}) collective-permute-start(bf16[4,64,512]{2,1,0:T(8,128)(2,1)S(1)} %get-tuple-element.38), channel_id=1, source_target_pairs={{0,4},{4,0},{8,12},{12,8},{16,20},{20,16},{24,28},{28,24},{1,5},{5... | collective-permute-start | bytes 786440 | tf_op jit(solution)/shard_map/ppermute | solution.py:23
  55.9 12.4 %collective-permute-start.18 = (bf16[4,64,512]{2,1,0:T(8,128)(2,1)S(1)}, bf16[4,64,512]{2,1,0:T(8,128)(2,1)S(1)}, u32[]{:S(2)}, u32[]{:S(2)}) collective-permute-start(bf16[4,64,512]{2,1,0:T(8,128)(2,1)S(1)} %get-tuple-element.40), channel_id=1, source_target_pairs={{0,4},{4,0},{8,12},{12,8},{16,20},{20,16},{24,28},{28,24},{1,5},{5... | collective-permute-start | bytes 786440 | tf_op jit(solution)/shard_map/ppermute | solution.py:23
  63.6 7.0 %collective-permute-start.15 = (bf16[64,512]{1,0:T(8,128)(2,1)S(1)}, bf16[64,512]{1,0:T(8,128)(2,1)S(1)}, u32[]{:S(2)}, u32[]{:S(2)}) collective-permute-start(bf16[64,512]{1,0:T(8,128)(2,1)S(1)} %get-tuple-element.51), channel_id=1, source_target_pairs={{0,8},{4,12},{8,0},{12,4},{16,24},{20,28},{24,16},{28,20},{1,9},{5... | collective-permute-start | bytes 196616 | tf_op jit(solution)/shard_map/ppermute | solution.py:23
  65.2 7.7 %collective-permute-start.16 = (bf16[64,512]{1,0:T(8,128)(2,1)S(1)}, bf16[64,512]{1,0:T(8,128)(2,1)S(1)}, u32[]{:S(2)}, u32[]{:S(2)}) collective-permute-start(bf16[64,512]{1,0:T(8,128)(2,1)S(1)} %get-tuple-element.53), channel_id=1, source_target_pairs={{0,16},{4,20},{8,24},{12,28},{16,0},{20,4},{24,8},{28,12},{1,17},{... | collective-permute-start | bytes 196616 | tf_op jit(solution)/shard_map/ppermute | solution.py:23
  65.6 7.2 %collective-permute-start.17 = (bf16[64,512]{1,0:T(8,128)(2,1)S(1)}, bf16[64,512]{1,0:T(8,128)(2,1)S(1)}, u32[]{:S(2)}, u32[]{:S(2)}) collective-permute-start(bf16[64,512]{1,0:T(8,128)(2,1)S(1)} %get-tuple-element.52), channel_id=1, source_target_pairs={{0,24},{4,28},{8,16},{12,20},{16,8},{20,12},{24,0},{28,4},{1,25},{... | collective-permute-start | bytes 196616 | tf_op jit(solution)/shard_map/ppermute | solution.py:23
  69.9 7.4 %collective-permute-start.20 = (bf16[64,512]{1,0:T(8,128)(2,1)S(1)}, bf16[64,512]{1,0:T(8,128)(2,1)S(1)}, u32[]{:S(2)}, u32[]{:S(2)}) collective-permute-start(bf16[64,512]{1,0:T(8,128)(2,1)S(1)} %get-tuple-element.56), channel_id=1, source_target_pairs={{0,16},{4,20},{8,24},{12,28},{16,0},{20,4},{24,8},{28,12},{1,17},{... | collective-permute-start | bytes 196616 | tf_op jit(solution)/shard_map/ppermute | solution.py:23
  70.6 6.7 %collective-permute-start.21 = (bf16[64,512]{1,0:T(8,128)(2,1)S(1)}, bf16[64,512]{1,0:T(8,128)(2,1)S(1)}, u32[]{:S(2)}, u32[]{:S(2)}) collective-permute-start(bf16[64,512]{1,0:T(8,128)(2,1)S(1)} %get-tuple-element.55), channel_id=1, source_target_pairs={{0,24},{4,28},{8,16},{12,20},{16,8},{20,12},{24,0},{28,4},{1,25},{... | collective-permute-start | bytes 196616 | tf_op jit(solution)/shard_map/ppermute | solution.py:23
  79.2 12.1 %all-to-all-start = ((bf16[8,32,512]{2,1,0:T(8,128)(2,1)}), bf16[8,32,512]{2,1,0:T(8,128)(2,1)S(1)}, u32[]{:S(2)}, u32[]{:S(2)}) async-start(bf16[8,32,512]{2,1,0:T(8,128)(2,1)} %bitcast.22), calls=%async_computation | async-start | bytes 524288 | tf_op jit(solution)/shard_map/all_to_all | solution.py:501
  91.7 6.4 %collective-permute-start.22 = (bf16[32,4096]{1,0:T(8,128)(2,1)S(1)}, bf16[32,4096]{1,0:T(8,128)(2,1)S(1)}, u32[]{:S(2)}, u32[]{:S(2)}) collective-permute-start(bf16[32,4096]{1,0:T(8,128)(2,1)S(1)} %normed_rows.2.refs_0_), channel_id=1, source_target_pairs={{0,2},{1,3},{2,0},{3,1},{4,6},{5,7},{6,4},{7,5},{8,10},{9,11},{10,... | collective-permute-start | bytes 786440 | tf_op jit(solution)/shard_map/ppermute | solution.py:23
  93.5 23.2 %all-to-all-start.1 = ((bf16[8,32,512]{2,1,0:T(8,128)(2,1)}), bf16[8,32,512]{2,1,0:T(8,128)(2,1)S(1)}, u32[]{:S(2)}, u32[]{:S(2)}) async-start(bf16[8,32,512]{2,1,0:T(8,128)(2,1)} %bitcast.26), calls=%async_computation.1 | async-start | bytes 524288 | tf_op jit(solution)/shard_map/all_to_all | solution.py:501
  116.4 9.3 %collective-permute-start.25 = (bf16[64,4096]{1,0:T(8,128)(2,1)S(1)}, bf16[64,4096]{1,0:T(8,128)(2,1)S(1)}, u32[]{:S(2)}, u32[]{:S(2)}) collective-permute-start(bf16[64,4096]{1,0:T(8,128)(2,1)S(1)} %get-tuple-element.44), channel_id=1, source_target_pairs={{0,1},{1,0},{2,3},{3,2},{4,5},{5,4},{6,7},{7,6},{8,9},{9,8},{10,11... | collective-permute-start | bytes 1572872 | tf_op jit(solution)/shard_map/ppermute | solution.py:23
  117.0 8.7 %collective-permute-start.27 = (bf16[32,4096]{1,0:T(8,128)(2,1)S(1)}, bf16[32,4096]{1,0:T(8,128)(2,1)S(1)}, u32[]{:S(2)}, u32[]{:S(2)}) collective-permute-start(bf16[32,4096]{1,0:T(8,128)(2,1)S(1)} %normed_rows.3.refs_0_), channel_id=1, source_target_pairs={{0,2},{1,3},{2,0},{3,1},{4,6},{5,7},{6,4},{7,5},{8,10},{9,11},{10,... | collective-permute-start | bytes 786440 | tf_op jit(solution)/shard_map/ppermute | solution.py:23
  117.9 7.9 %collective-permute-start.28 = (bf16[32,4096]{1,0:T(8,128)(2,1)S(1)}, bf16[32,4096]{1,0:T(8,128)(2,1)S(1)}, u32[]{:S(2)}, u32[]{:S(2)}) collective-permute-start(bf16[32,4096]{1,0:T(8,128)(2,1)S(1)} %normed_rows.3.refs_0_), channel_id=1, source_target_pairs={{0,1},{1,0},{2,3},{3,2},{4,5},{5,4},{6,7},{7,6},{8,9},{9,8},{10,11... | collective-permute-start | bytes 786440 | tf_op jit(solution)/shard_map/ppermute | solution.py:23
  144.4 9.2 %collective-permute-start.26 = (bf16[32,4096]{1,0:T(8,128)(2,1)S(1)}, bf16[32,4096]{1,0:T(8,128)(2,1)S(1)}, u32[]{:S(2)}, u32[]{:S(2)}) collective-permute-start(bf16[32,4096]{1,0:T(8,128)(2,1)S(1)} %slice.235), channel_id=1, source_target_pairs={{0,2},{1,3},{2,0},{3,1},{4,6},{5,7},{6,4},{7,5},{8,10},{9,11},{10,... | collective-permute-start | bytes 786440 | tf_op jit(solution)/shard_map/ppermute | solution.py:23
  146.0 12.7 %collective-permute-start.31 = (bf16[32,4096]{1,0:T(8,128)(2,1)S(1)}, bf16[32,4096]{1,0:T(8,128)(2,1)S(1)}, u32[]{:S(2)}, u32[]{:S(2)}) collective-permute-start(bf16[32,4096]{1,0:T(8,128)(2,1)S(1)} %slice.234), channel_id=1, source_target_pairs={{0,2},{1,3},{2,0},{3,1},{4,6},{5,7},{6,4},{7,5},{8,10},{9,11},{10,... | collective-permute-start | bytes 786440 | tf_op jit(solution)/shard_map/ppermute | solution.py:23
  (20 other events, 148.1 us)
